TPU v7x, 256 devices: a whole 4x4x8 slice. The times are simulated.
256 devices in a mesh: depth: 8 (over x, z_lo), map: 32 (over z_hi, y, core).
Axes of the slice: x: 4, y: 4, z: 8 (z_hi: 4, z_lo: 2; z = z_hi * 2 + z_lo), core: 2. Of those that a mesh axis runs over, the one named last changes fastest.
Arguments:
- velocity: float32 [3, 128, 1024, 128], P(None, 'depth', 'map'), may hold values from -6 to 6
- stress: float32 [6, 128, 1024, 128], P(None, 'depth', 'map'), may hold values from -6 to 6
- region: int32 [128, 1024, 128], P('depth', 'map'), may hold values from 0 to 7
- lame_table: float32 [8], replicated, may hold values from 0.2 to 0.5
- shear_table: float32 [8], replicated, may hold values from 0.1 to 0.3
- buoyancy_table: float32 [8], replicated, may hold values from 0.6 to 1.2
- height: float32 [1024, 8192], P('depth', 'map'), may hold values from -6 to 6
- discharge: float32 [2, 1024, 8192], P(None, 'depth', 'map'), may hold values from -6 to 6
- face_depth: float32 [2, 1024, 8192], P(None, 'depth', 'map'), may hold values from 0.5 to 2
- wet: int32 [1024, 8192], P('depth', 'map'), may hold values 0 or 1
- seafloor_index: int32 [1024, 8192], P('depth', 'map'), may hold values from 0 to 4095
Outputs:
- velocity_out: float32 [3, 128, 1024, 128], P(None, 'depth', 'map')
- stress_out: float32 [6, 128, 1024, 128], P(None, 'depth', 'map')
- height_out: float32 [1024, 8192], P('depth', 'map')
- discharge_out: float32 [2, 1024, 8192], P(None, 'depth', 'map')
Inputs may be any that keep to these rules, and one draw needn't show every extreme that they name: `wet`: 1 for a wet ocean cell, 0 for a dry one. `seafloor_index`: index k of the seafloor cell under an ocean cell, among the 32 x 128 crust cells of its own map column, counted row by row.
All inputs are finite; a program needn't handle non-finite values. No bound on the sum of `wet` on one device may be relied on, other than what follows from the above.
Results may differ from a plain program's by a relative error of at most 0.000054.
Values sent between devices are 32-bit elements; how exact they have to be, the bound alone decides.
A program may use at most 64 MiB of HBM per device.

v0:
```python
import math

import jax
import jax.numpy as jnp
from jax import lax
from jax.sharding import PartitionSpec as P

ITERS = 3
OSTEPS = 2


near_coef = 9.0 / 8.0
far_coef = 1.0 / 24.0
time_step = 0.2
ocean_step = 0.2
gravity = 1.0


def with_halo(x, sides, width):
    edges = {}
    for axis, dim in sides:
        peers, length = (lax.axis_size(axis), x.shape[dim])
        up = [(i, (i + 1) % peers) for i in range(peers - 1)]
        last = lax.slice_in_dim(x, length - width, length, axis=dim)
        leading = lax.slice_in_dim(x, 0, width, axis=dim)
        edges[dim] = (
            lax.ppermute(last, axis, up),
            lax.ppermute(leading, axis, [(b, a) for a, b in up]),
        )
    done = []
    for _, dim in sides:
        low, high = edges[dim]
        around = [(width, width) if d in done else (0, 0) for d in range(x.ndim)]
        x = jnp.concatenate([jnp.pad(low, around), x, jnp.pad(high, around)], axis=dim)
        done.append(dim)
    return x


def from_root(x, axis, root):
    return lax.dynamic_index_in_dim(lax.all_gather(x, axis), root, 0, keepdims=False)


def passed_along(x, axis, by):
    peers = lax.axis_size(axis)
    pairs = [(i, i + by) for i in range(peers) if 0 <= i + by < peers]
    return lax.ppermute(x, axis, pairs)


def cells(padded, axis, offset, count):
    return lax.slice_in_dim(padded, offset, offset + count, axis=axis)


def forward_diff(padded, axis):
    count = padded.shape[axis] - 4
    return near_coef * (
        cells(padded, axis, 3, count) - cells(padded, axis, 2, count)
    ) - far_coef * (cells(padded, axis, 4, count) - cells(padded, axis, 1, count))


def backward_diff(padded, axis):
    count = padded.shape[axis] - 4
    return near_coef * (
        cells(padded, axis, 2, count) - cells(padded, axis, 1, count)
    ) - far_coef * (cells(padded, axis, 3, count) - cells(padded, axis, 0, count))


def forward_y(field):
    return near_coef * (jnp.roll(field, -1, 2) - field) - far_coef * (
        jnp.roll(field, -2, 2) - jnp.roll(field, 1, 2)
    )


def backward_y(field):
    return near_coef * (field - jnp.roll(field, 1, 2)) - far_coef * (
        jnp.roll(field, -1, 2) - jnp.roll(field, 2, 2)
    )


def lookup(region, table):
    total = jnp.zeros(region.shape, jnp.float32)
    for value in range(table.shape[0]):
        total = total + jnp.where(region == value, table[value], 0.0)
    return total


def seafloor_pick(tiles, seafloor_index):
    tile_rows = tiles.shape[1]
    tile_cols = tiles.shape[2]
    ocean_rows = seafloor_index.shape[0]
    ocean_cols = seafloor_index.shape[1]
    group = math.gcd(ocean_rows, 8)
    table = jnp.transpose(tiles, (1, 0, 2)).reshape(tile_rows, 2 * tile_cols)
    row_ids = lax.broadcasted_iota(jnp.int32, (1, 1, tile_rows), 2)
    col_ids = lax.broadcasted_iota(jnp.int32, (1, 1, tile_cols), 2)

    def one_block(indices):
        upper = indices // tile_cols
        lower = indices % tile_cols
        onehot = (upper[:, :, None] == row_ids).astype(jnp.float32)
        picked = jnp.einsum("rck,kn->rcn", onehot, table, precision=lax.Precision.HIGHEST)
        chosen = lower[:, :, None] == col_ids
        first = jnp.sum(jnp.where(chosen, picked[:, :, :tile_cols], 0.0), axis=2)
        second = jnp.sum(jnp.where(chosen, picked[:, :, tile_cols:], 0.0), axis=2)
        return jnp.stack([first, second])

    blocks = seafloor_index.reshape(ocean_rows // group, group, ocean_cols)
    result = lax.map(one_block, blocks)
    result = jnp.transpose(result, (1, 0, 2, 3)).reshape(2, ocean_rows, ocean_cols)
    return (result[0], result[1])


def per_device(
    velocity,
    stress,
    region,
    lame_table,
    shear_table,
    buoyancy_table,
    height,
    discharge,
    face_depth,
    wet,
    seafloor_index,
):
    lame = lookup(region, lame_table)
    shear = lookup(region, shear_table)
    buoyancy = lookup(region, buoyancy_table)
    speeds = velocity
    forces = stress
    lift = jnp.zeros((velocity.shape[2], velocity.shape[3]), jnp.float32)
    for turn in range(ITERS):
        padded = with_halo(forces, (("depth", 1), ("map", 2)), 2)
        map_part = padded[:, 2:-2]
        depth_part = padded[:, :, 2:-2][2:5]
        speed_x = speeds[0] + time_step * buoyancy * (
            forward_diff(map_part[0], 1) + backward_y(forces[1]) + backward_diff(depth_part[0], 0)
        )
        speed_y = speeds[1] + time_step * buoyancy * (
            backward_diff(map_part[1], 1) + forward_y(forces[5]) + backward_diff(depth_part[1], 0)
        )
        speed_z = speeds[2] + time_step * buoyancy * (
            backward_diff(map_part[2], 1) + backward_y(forces[3]) + forward_diff(depth_part[2], 0)
        )
        speeds = jnp.stack([speed_x, speed_y, speed_z])
        lift = lift + time_step * speed_z[0]
        beside_all = with_halo(speeds, (("depth", 1), ("map", 2)), 2)
        speed_map = beside_all[:, 2:-2]
        speed_depth = beside_all[:, :, 2:-2]
        strain_x = backward_diff(speed_map[0], 1)
        strain_y = backward_y(speed_y)
        strain_z = backward_diff(speed_depth[2], 0)
        spread = strain_x + strain_y + strain_z
        forces = jnp.stack(
            [
                forces[0] + time_step * (lame * spread + 2.0 * shear * strain_x),
                forces[1]
                + time_step * shear * (forward_y(speed_x) + forward_diff(speed_map[1], 1)),
                forces[2]
                + time_step
                * shear
                * (forward_diff(speed_depth[0], 0) + forward_diff(speed_map[2], 1)),
                forces[3]
                + time_step * shear * (forward_diff(speed_depth[1], 0) + forward_y(speed_z)),
                forces[4] + time_step * (lame * spread + 2.0 * shear * strain_z),
                forces[5] + time_step * (lame * spread + 2.0 * shear * strain_y),
            ]
        )
    tiles = from_root(jnp.stack([lift, speeds[2][0]]), "depth", 0)
    lift_at, rate_at = seafloor_pick(tiles, seafloor_index)
    wetness = wet.astype(jnp.float32)
    level = wetness * (height + lift_at)
    source = wetness * rate_at
    east_pair = passed_along(jnp.stack([level[:, :1], wetness[:, :1]]), "map", -1)
    north_pair = passed_along(jnp.stack([level[:1, :], wetness[:1, :]]), "depth", -1)
    wet_east = jnp.concatenate([wetness[:, 1:], east_pair[1]], axis=1)
    wet_north = jnp.concatenate([wetness[1:, :], north_pair[1]], axis=0)
    mask_x = wetness * wet_east
    mask_y = wetness * wet_north
    depth_x = face_depth[0] * mask_x
    depth_y = face_depth[1] * mask_y
    flux_x = discharge[0] * mask_x
    flux_y = discharge[1] * mask_y
    for turn in range(OSTEPS):
        if turn == 0:
            east_col = east_pair[0]
            north_row = north_pair[0]
        else:
            east_col = passed_along(level[:, :1], "map", -1)
            north_row = passed_along(level[:1, :], "depth", -1)
        level_east = jnp.concatenate([level[:, 1:], east_col], axis=1)
        level_north = jnp.concatenate([level[1:, :], north_row], axis=0)
        flux_x = flux_x - ocean_step * gravity * depth_x * (level_east - level)
        flux_y = flux_y - ocean_step * gravity * depth_y * (level_north - level)
        west_col = passed_along(flux_x[:, -1:], "map", 1)
        south_row = passed_along(flux_y[-1:, :], "depth", 1)
        flux_west = jnp.concatenate([west_col, flux_x[:, :-1]], axis=1)
        flux_south = jnp.concatenate([south_row, flux_y[:-1, :]], axis=0)
        level = (
            level
            - ocean_step * wetness * (flux_x - flux_west + (flux_y - flux_south))
            + ocean_step * source
        )
    return (speeds, forces, level, jnp.stack([flux_x, flux_y]))


def solution(mesh):
    return jax.shard_map(
        per_device,
        mesh=mesh,
        in_specs=(
            P(None, "depth", "map", None),
            P(None, "depth", "map", None),
            P("depth", "map", None),
            P(),
            P(),
            P(),
            P("depth", "map"),
            P(None, "depth", "map"),
            P(None, "depth", "map"),
            P("depth", "map"),
            P("depth", "map"),
        ),
        out_specs=(
            P(None, "depth", "map", None),
            P(None, "depth", "map", None),
            P("depth", "map"),
            P(None, "depth", "map"),
        ),
        check_vma=False,
    )
```

profile of v0, /device:TPU:121, one launch (start us, length us, event | category | flops | bytes accessed | tf_op | source)
XLA Modules:
  0.0 294.1 jit_solution(9696544882120657969)
XLA Ops:
  2.4 2.7 collective-permute-start.1
  5.1 3.3 %collective-permute-start.2 = (f32[6,2,32,128]{3,2,1,0:T(8,128)}, f32[6,2,32,128]{3,2,1,0:T(8,128)S(1)}, u32[]{:S(2)}, u32[]{:S(2)}) collective-permute-start(f32[6,2,32,128]{3,2,1,0:T(8,128)} %get-tuple-element.176), channel_id=1, source_target_pairs={{32,0},{64,32},{96,64},{128,96},{160,128},{192,160},{224,192},{33,... | collective-permute-start | bytes 589832 | tf_op jit(solution)/shard_map/ppermute | solution.py:28
  10.2 6.0 %collective-permute-start = (f32[6,16,2,128]{3,2,1,0:T(2,128)}, f32[6,16,2,128]{3,2,1,0:T(2,128)}, u32[]{:S(2)}, u32[]{:S(2)}) collective-permute-start(f32[6,16,2,128]{3,2,1,0:T(2,128)} %get-tuple-element.174), channel_id=1, source_target_pairs={{0,1},{1,2},{2,3},{3,4},{4,5},{5,6},{6,7},{7,8},{8,9},{9,10},{10,1... | collective-permute-start | bytes 294920 | tf_op jit(solution)/shard_map/ppermute | solution.py:27
  16.2 1.9 collective-permute-start.3
  32.1 6.0 %fusion.220 = (f32[16,32,128]{2,1,0:T(8,128)S(1)}, f32[16,32,128]{2,1,0:T(8,128)S(1)}, pred[16,32,128]{2,1,0:T(8,128)(4,1)S(1)}, pred[16,32,128]{2,1,0:T(8,128)(...) fusion(f32[6,18,32,128]{3,2,1,0:T(8,128)S(1)} %get-tuple-elemen, ...), kind=kLoop, calls=%fused_computation.343 | loop fusion | flops 3014656 | bytes 4718624 | tf_op jit(solution)/shard_map/add | solution.py:135
  40.6 7.9 %collective-permute-start.4 = (f32[3,16,2,128]{3,2,1,0:T(2,128)S(1)}, f32[3,16,2,128]{3,2,1,0:T(2,128)S(1)}, u32[]{:S(2)}, u32[]{:S(2)}) collective-permute-start(f32[3,16,2,128]{3,2,1,0:T(2,128)S(1)} %get-tuple-element.207), channel_id=1, source_target_pairs={{0,1},{1,2},{2,3},{3,4},{4,5},{5,6},{6,7},{7,8},{8,9},{9,10},{10,1... | collective-permute-start | bytes 147464 | tf_op jit(solution)/shard_map/ppermute | solution.py:27
  50.4 3.8 %collective-permute-start.5 = (f32[3,2,32,128]{3,2,1,0:T(8,128)S(1)}, f32[3,2,32,128]{3,2,1,0:T(8,128)S(1)}, u32[]{:S(2)}, u32[]{:S(2)}) collective-permute-start(f32[3,2,32,128]{3,2,1,0:T(8,128)S(1)} %get-tuple-element.205), channel_id=1, source_target_pairs={{0,32},{32,64},{64,96},{96,128},{128,160},{160,192},{192,224},{1,3... | collective-permute-start | bytes 294920 | tf_op jit(solution)/shard_map/ppermute | solution.py:27
  58.5 1.9 collective-permute-done.6
  60.9 10.7 %bitcast_dynamic-update-slice_fusion.14 = (f32[6,16,32,128]{3,2,1,0:T(8,128)S(1)}, f32[16,32,128]{2,1,0:T(8,128)S(1)}, f32[16,32,128]{2,1,0:T(8,128)S(1)}, f32[1...) fusion(f32[6,16,32,128]{3,2,1,0:T(8,128)S(1)} %copy-done, ...), kind=kLoop, calls=%fused_computation.458 | loop fusion | flops 3670015 | bytes 5767232
  75.4 4.3 %collective-permute-start.9 = (f32[6,2,32,128]{3,2,1,0:T(8,128)S(1)}, f32[6,2,32,128]{3,2,1,0:T(8,128)S(1)}, u32[]{:S(2)}, u32[]{:S(2)}) collective-permute-start(f32[6,2,32,128]{3,2,1,0:T(8,128)S(1)} %get-tuple-element.170), channel_id=1, source_target_pairs={{0,32},{32,64},{64,96},{96,128},{128,160},{160,192},{192,224},{1,3... | collective-permute-start | bytes 589832 | tf_op jit(solution)/shard_map/ppermute | solution.py:27
  81.6 9.9 %collective-permute-start.8 = (f32[6,16,2,128]{3,2,1,0:T(2,128)S(1)}, f32[6,16,2,128]{3,2,1,0:T(2,128)S(1)}, u32[]{:S(2)}, u32[]{:S(2)}) collective-permute-start(f32[6,16,2,128]{3,2,1,0:T(2,128)S(1)} %get-tuple-element.167), channel_id=1, source_target_pairs={{0,1},{1,2},{2,3},{3,4},{4,5},{5,6},{6,7},{7,8},{8,9},{9,10},{10,1... | collective-permute-start | bytes 294920 | tf_op jit(solution)/shard_map/ppermute | solution.py:27
  97.5 3.4 %collective-permute-start.14 = (f32[3,2,32,128]{3,2,1,0:T(8,128)S(1)}, f32[3,2,32,128]{3,2,1,0:T(8,128)S(1)}, u32[]{:S(2)}, u32[]{:S(2)}) collective-permute-start(f32[3,2,32,128]{3,2,1,0:T(8,128)S(1)} %get-tuple-element.200), channel_id=1, source_target_pairs={{32,0},{64,32},{96,64},{128,96},{160,128},{192,160},{224,192},{33,... | collective-permute-start | bytes 294920 | tf_op jit(solution)/shard_map/ppermute | solution.py:28
  100.9 9.1 %collective-permute-start.12 = (f32[3,16,2,128]{3,2,1,0:T(2,128)S(1)}, f32[3,16,2,128]{3,2,1,0:T(2,128)S(1)}, u32[]{:S(2)}, u32[]{:S(2)}) collective-permute-start(f32[3,16,2,128]{3,2,1,0:T(2,128)S(1)} %get-tuple-element.201), channel_id=1, source_target_pairs={{0,1},{1,2},{2,3},{3,4},{4,5},{5,6},{6,7},{7,8},{8,9},{9,10},{10,1... | collective-permute-start | bytes 147464 | tf_op jit(solution)/shard_map/ppermute | solution.py:27
  110.0 2.1 collective-permute-start.15
  112.6 7.0 %collective-permute-done.15 = f32[3,16,2,128]{3,2,1,0:T(2,128)S(1)} collective-permute-done((f32[3,16,2,128]{3,2,1,0:T(2,128)S(1)}, f32[3,16,2,128]{3,2,1,0:T(2,128)S(1)}, u32[]{:S(2)}, u32[]{:S(2)}) %collective-permute-start.15) | collective-permute-done | bytes 49184 | tf_op jit(solution)/shard_map/ppermute | solution.py:28
  125.2 2.7 collective-permute-start.17
  128.0 2.5 collective-permute-start.18
  130.5 2.5 collective-permute-start.16
  138.5 4.7 %collective-permute-done.19 = f32[6,16,2,128]{3,2,1,0:T(2,128)S(1)} collective-permute-done((f32[6,16,2,128]{3,2,1,0:T(2,128)S(1)}, f32[6,16,2,128]{3,2,1,0:T(2,128)S(1)}, u32[]{:S(2)}, u32[]{:S(2)}) %collective-permute-start.19) | collective-permute-done | bytes 98336 | tf_op jit(solution)/shard_map/ppermute | solution.py:28
  144.9 21.1 %all-gather = f32[16,32,128]{2,1,0:T(8,128)S(1)} all-gather(f32[2,32,128]{2,1,0:T(8,128)S(1)} %pad_maximum_fusion.19), channel_id=2, replica_groups=mesh['depth'=8,'map'=32] {'depth'}, dimensions={0}, use_global_device_ids=true | all-gather | bytes 294912 | tf_op jit(solution)/shard_map/all_gather | solution.py:40
  166.0 52.3 %while.13 = (s32[]{:T(128)}, f32[16,2,8,256]{3,2,1,0:T(8,128)}, s32[16,8,256]{2,1,0:T(8,128)}, f32[32,256]{1,0:T(8,128)S(1)}, s32[]{:T(128)}) while((s32[]{:T(128)}, f32[16,2,8,256]{3,2,1,0:T(8,128)}, s32[16,8,256]{2,1,0:T(8,128)}, f32[32,256]{1,0:T(8,128)S(1)}, s32[]{:T(128)}) %tuple.170), condition=%wide.region_3.4_spmd.clone, body=%wide.region_0.3_spmd.clone.sunk | while | flops 202754048 | bytes 4330053 | solution.py:107
  219.4 2.5 fusion.69
  227.0 3.4 %collective-permute-start.24 = (f32[2,128,1]{1,2,0:T(1,128)S(1)}, f32[2,128,1]{1,2,0:T(1,128)S(1)}, u32[]{:S(2)}, u32[]{:S(2)}) collective-permute-start(f32[2,128,1]{1,2,0:T(1,128)S(1)} %pad_maximum_fusion.21), channel_id=1, source_target_pairs={{1,0},{2,1},{3,2},{4,3},{5,4},{6,5},{7,6},{8,7},{9,8},{10,9},{11,1... | collective-permute-start | bytes 3080 | tf_op jit(solution)/shard_map/ppermute | solution.py:46
  230.4 4.4 %collective-permute-start.26 = (f32[2,1,256]{2,1,0:T(1,128)S(1)}, f32[2,1,256]{2,1,0:T(1,128)S(1)}, u32[]{:S(2)}, u32[]{:S(2)}) collective-permute-start(f32[2,1,256]{2,1,0:T(1,128)S(1)} %pad_maximum_fusion.20), channel_id=1, source_target_pairs={{32,0},{64,32},{96,64},{128,96},{160,128},{192,160},{224,192},{33,... | collective-permute-start | bytes 6152 | tf_op jit(solution)/shard_map/ppermute | solution.py:46
  239.0 7.1 %collective-permute-start.25 = (f32[128,1]{1,0:T(8,128)S(1)}, f32[128,1]{1,0:T(8,128)S(1)}, u32[]{:S(2)}, u32[]{:S(2)}) collective-permute-start(f32[128,1]{1,0:T(8,128)S(1)} %slice.2008), channel_id=1, source_target_pairs={{0,1},{1,2},{2,3},{3,4},{4,5},{5,6},{6,7},{7,8},{8,9},{9,10},{10,1... | collective-permute-start | bytes 1544 | tf_op jit(solution)/shard_map/ppermute | solution.py:46
  246.1 2.0 collective-permute-start.27
  248.2 2.2 collective-permute-done.27
  255.9 4.3 %collective-permute-start.21 = (f32[3,2,32,128]{3,2,1,0:T(8,128)S(1)}, f32[3,2,32,128]{3,2,1,0:T(8,128)S(1)}, u32[]{:S(2)}, u32[]{:S(2)}) collective-permute-start(f32[3,2,32,128]{3,2,1,0:T(8,128)S(1)} %get-tuple-element.193), channel_id=1, source_target_pairs={{0,32},{32,64},{64,96},{96,128},{128,160},{160,192},{192,224},{1,3... | collective-permute-start | bytes 294920 | tf_op jit(solution)/shard_map/ppermute | solution.py:27
  262.1 8.1 %collective-permute-start.20 = (f32[3,16,2,128]{3,2,1,0:T(2,128)S(1)}, f32[3,16,2,128]{3,2,1,0:T(2,128)S(1)}, u32[]{:S(2)}, u32[]{:S(2)}) collective-permute-start(f32[3,16,2,128]{3,2,1,0:T(2,128)S(1)} %get-tuple-element.195), channel_id=1, source_target_pairs={{0,1},{1,2},{2,3},{3,4},{4,5},{5,6},{6,7},{7,8},{8,9},{9,10},{10,1... | collective-permute-start | bytes 147464 | tf_op jit(solution)/shard_map/ppermute | solution.py:27
  272.5 4.5 %collective-permute-start.31 = (f32[1,256]{1,0:T(1,128)S(1)}, f32[1,256]{1,0:T(1,128)S(1)}, u32[]{:S(2)}, u32[]{:S(2)}) collective-permute-start(f32[1,256]{1,0:T(1,128)S(1)} %slice.2025), channel_id=1, source_target_pairs={{0,32},{32,64},{64,96},{96,128},{128,160},{160,192},{192,224},{1,3... | collective-permute-start | bytes 3080 | tf_op jit(solution)/shard_map/ppermute | solution.py:46
  277.8 2.7 collective-permute-start.23
  282.2 5.2 %collective-permute-done.23 = f32[3,16,2,128]{3,2,1,0:T(2,128)S(1)} collective-permute-done((f32[3,16,2,128]{3,2,1,0:T(2,128)S(1)}, f32[3,16,2,128]{3,2,1,0:T(2,128)S(1)}, u32[]{:S(2)}, u32[]{:S(2)}) %collective-permute-start.23) | collective-permute-done | bytes 49184 | tf_op jit(solution)/shard_map/ppermute | solution.py:28
  (391 shorter events, 131.8 us)
Async XLA Ops:
  2.4 25.6 %collective-permute-start.1 = (f32[6,2,32,128]{3,2,1,0:T(8,128)}, f32[6,2,32,128]{3,2,1,0:T(8,128)}, u32[]{:S(2)}, u32[]{:S(2)}) collective-permute-start(f32[6,2,32,128]{3,2,1,0:T(8,128)} %get-tuple-element.177), channel_id=1, source_target_pairs={{0,32},{32,64},{64,96},{96,128},{128,160},{160,192},{192,224},{1,3... | collective-permute-start | bytes 589832 | tf_op jit(solution)/shard_map/ppermute | solution.py:27
  5.1 23.0 %collective-permute-start.2 = (f32[6,2,32,128]{3,2,1,0:T(8,128)}, f32[6,2,32,128]{3,2,1,0:T(8,128)S(1)}, u32[]{:S(2)}, u32[]{:S(2)}) collective-permute-start(f32[6,2,32,128]{3,2,1,0:T(8,128)} %get-tuple-element.176), channel_id=1, source_target_pairs={{32,0},{64,32},{96,64},{128,96},{160,128},{192,160},{224,192},{33,... | collective-permute-start | bytes 589832 | tf_op jit(solution)/shard_map/ppermute | solution.py:28
  10.2 17.8 %collective-permute-start = (f32[6,16,2,128]{3,2,1,0:T(2,128)}, f32[6,16,2,128]{3,2,1,0:T(2,128)}, u32[]{:S(2)}, u32[]{:S(2)}) collective-permute-start(f32[6,16,2,128]{3,2,1,0:T(2,128)} %get-tuple-element.174), channel_id=1, source_target_pairs={{0,1},{1,2},{2,3},{3,4},{4,5},{5,6},{6,7},{7,8},{8,9},{9,10},{10,1... | collective-permute-start | bytes 294920 | tf_op jit(solution)/shard_map/ppermute | solution.py:27
  16.2 11.8 %collective-permute-start.3 = (f32[6,16,2,128]{3,2,1,0:T(2,128)S(1)}, f32[6,16,2,128]{3,2,1,0:T(2,128)}, u32[]{:S(2)}, u32[]{:S(2)}) collective-permute-start(f32[6,16,2,128]{3,2,1,0:T(2,128)S(1)} %get-tuple-element.175), channel_id=1, source_target_pairs={{1,0},{2,1},{3,2},{4,3},{5,4},{6,5},{7,6},{8,7},{9,8},{10,9},{11,1... | collective-permute-start | bytes 294920 | tf_op jit(solution)/shard_map/ppermute | solution.py:28
  40.6 16.1 %collective-permute-start.4 = (f32[3,16,2,128]{3,2,1,0:T(2,128)S(1)}, f32[3,16,2,128]{3,2,1,0:T(2,128)S(1)}, u32[]{:S(2)}, u32[]{:S(2)}) collective-permute-start(f32[3,16,2,128]{3,2,1,0:T(2,128)S(1)} %get-tuple-element.207), channel_id=1, source_target_pairs={{0,1},{1,2},{2,3},{3,4},{4,5},{5,6},{6,7},{7,8},{8,9},{9,10},{10,1... | collective-permute-start | bytes 147464 | tf_op jit(solution)/shard_map/ppermute | solution.py:27
  48.4 10.1 %collective-permute-start.7 = (f32[3,16,2,128]{3,2,1,0:T(2,128)S(1)}, f32[3,16,2,128]{3,2,1,0:T(2,128)S(1)}, u32[]{:S(2)}, u32[]{:S(2)}) collective-permute-start(f32[3,16,2,128]{3,2,1,0:T(2,128)S(1)} %get-tuple-element.208), channel_id=1, source_target_pairs={{1,0},{2,1},{3,2},{4,3},{5,4},{6,5},{7,6},{8,7},{9,8},{10,9},{11,1... | collective-permute-start | bytes 147464 | tf_op jit(solution)/shard_map/ppermute | solution.py:28
  50.4 8.1 %collective-permute-start.5 = (f32[3,2,32,128]{3,2,1,0:T(8,128)S(1)}, f32[3,2,32,128]{3,2,1,0:T(8,128)S(1)}, u32[]{:S(2)}, u32[]{:S(2)}) collective-permute-start(f32[3,2,32,128]{3,2,1,0:T(8,128)S(1)} %get-tuple-element.205), channel_id=1, source_target_pairs={{0,32},{32,64},{64,96},{96,128},{128,160},{160,192},{192,224},{1,3... | collective-permute-start | bytes 294920 | tf_op jit(solution)/shard_map/ppermute | solution.py:27
  54.2 6.3 %collective-permute-start.6 = (f32[3,2,32,128]{3,2,1,0:T(8,128)S(1)}, f32[3,2,32,128]{3,2,1,0:T(8,128)S(1)}, u32[]{:S(2)}, u32[]{:S(2)}) collective-permute-start(f32[3,2,32,128]{3,2,1,0:T(8,128)S(1)} %get-tuple-element.206), channel_id=1, source_target_pairs={{32,0},{64,32},{96,64},{128,96},{160,128},{192,160},{224,192},{33,... | collective-permute-start | bytes 294920 | tf_op jit(solution)/shard_map/ppermute | solution.py:28
  73.5 19.6 %collective-permute-start.10 = (f32[6,2,32,128]{3,2,1,0:T(8,128)S(1)}, f32[6,2,32,128]{3,2,1,0:T(8,128)S(1)}, u32[]{:S(2)}, u32[]{:S(2)}) collective-permute-start(f32[6,2,32,128]{3,2,1,0:T(8,128)S(1)} %get-tuple-element.169), channel_id=1, source_target_pairs={{32,0},{64,32},{96,64},{128,96},{160,128},{192,160},{224,192},{33,... | collective-permute-start | bytes 589832 | tf_op jit(solution)/shard_map/ppermute | solution.py:28
  75.4 17.7 %collective-permute-start.9 = (f32[6,2,32,128]{3,2,1,0:T(8,128)S(1)}, f32[6,2,32,128]{3,2,1,0:T(8,128)S(1)}, u32[]{:S(2)}, u32[]{:S(2)}) collective-permute-start(f32[6,2,32,128]{3,2,1,0:T(8,128)S(1)} %get-tuple-element.170), channel_id=1, source_target_pairs={{0,32},{32,64},{64,96},{96,128},{128,160},{160,192},{192,224},{1,3... | collective-permute-start | bytes 589832 | tf_op jit(solution)/shard_map/ppermute | solution.py:27
  79.7 12.5 %collective-permute-start.11 = (f32[6,16,2,128]{3,2,1,0:T(2,128)S(1)}, f32[6,16,2,128]{3,2,1,0:T(2,128)S(1)}, u32[]{:S(2)}, u32[]{:S(2)}) collective-permute-start(f32[6,16,2,128]{3,2,1,0:T(2,128)S(1)} %get-tuple-element.168), channel_id=1, source_target_pairs={{1,0},{2,1},{3,2},{4,3},{5,4},{6,5},{7,6},{8,7},{9,8},{10,9},{11,1... | collective-permute-start | bytes 294920 | tf_op jit(solution)/shard_map/ppermute | solution.py:28
  81.6 11.5 %collective-permute-start.8 = (f32[6,16,2,128]{3,2,1,0:T(2,128)S(1)}, f32[6,16,2,128]{3,2,1,0:T(2,128)S(1)}, u32[]{:S(2)}, u32[]{:S(2)}) collective-permute-start(f32[6,16,2,128]{3,2,1,0:T(2,128)S(1)} %get-tuple-element.167), channel_id=1, source_target_pairs={{0,1},{1,2},{2,3},{3,4},{4,5},{5,6},{6,7},{7,8},{8,9},{9,10},{10,1... | collective-permute-start | bytes 294920 | tf_op jit(solution)/shard_map/ppermute | solution.py:27
  95.6 24.0 %collective-permute-start.13 = (f32[3,2,32,128]{3,2,1,0:T(8,128)S(1)}, f32[3,2,32,128]{3,2,1,0:T(8,128)S(1)}, u32[]{:S(2)}, u32[]{:S(2)}) collective-permute-start(f32[3,2,32,128]{3,2,1,0:T(8,128)S(1)} %get-tuple-element.199), channel_id=1, source_target_pairs={{0,32},{32,64},{64,96},{96,128},{128,160},{160,192},{192,224},{1,3... | collective-permute-start | bytes 294920 | tf_op jit(solution)/shard_map/ppermute | solution.py:27
  97.5 22.1 %collective-permute-start.14 = (f32[3,2,32,128]{3,2,1,0:T(8,128)S(1)}, f32[3,2,32,128]{3,2,1,0:T(8,128)S(1)}, u32[]{:S(2)}, u32[]{:S(2)}) collective-permute-start(f32[3,2,32,128]{3,2,1,0:T(8,128)S(1)} %get-tuple-element.200), channel_id=1, source_target_pairs={{32,0},{64,32},{96,64},{128,96},{160,128},{192,160},{224,192},{33,... | collective-permute-start | bytes 294920 | tf_op jit(solution)/shard_map/ppermute | solution.py:28
  100.9 11.8 %collective-permute-start.12 = (f32[3,16,2,128]{3,2,1,0:T(2,128)S(1)}, f32[3,16,2,128]{3,2,1,0:T(2,128)S(1)}, u32[]{:S(2)}, u32[]{:S(2)}) collective-permute-start(f32[3,16,2,128]{3,2,1,0:T(2,128)S(1)} %get-tuple-element.201), channel_id=1, source_target_pairs={{0,1},{1,2},{2,3},{3,4},{4,5},{5,6},{6,7},{7,8},{8,9},{9,10},{10,1... | collective-permute-start | bytes 147464 | tf_op jit(solution)/shard_map/ppermute | solution.py:27
  110.0 9.6 %collective-permute-start.15 = (f32[3,16,2,128]{3,2,1,0:T(2,128)S(1)}, f32[3,16,2,128]{3,2,1,0:T(2,128)S(1)}, u32[]{:S(2)}, u32[]{:S(2)}) collective-permute-start(f32[3,16,2,128]{3,2,1,0:T(2,128)S(1)} %get-tuple-element.202), channel_id=1, source_target_pairs={{1,0},{2,1},{3,2},{4,3},{5,4},{6,5},{7,6},{8,7},{9,8},{10,9},{11,1... | collective-permute-start | bytes 147464 | tf_op jit(solution)/shard_map/ppermute | solution.py:28
  125.2 17.9 %collective-permute-start.17 = (f32[6,2,32,128]{3,2,1,0:T(8,128)S(1)}, f32[6,2,32,128]{3,2,1,0:T(8,128)S(1)}, u32[]{:S(2)}, u32[]{:S(2)}) collective-permute-start(f32[6,2,32,128]{3,2,1,0:T(8,128)S(1)} %get-tuple-element.166), channel_id=1, source_target_pairs={{0,32},{32,64},{64,96},{96,128},{128,160},{160,192},{192,224},{1,3... | collective-permute-start | bytes 589832 | tf_op jit(solution)/shard_map/ppermute | solution.py:27
  128.0 15.2 %collective-permute-start.18 = (f32[6,2,32,128]{3,2,1,0:T(8,128)S(1)}, f32[6,2,32,128]{3,2,1,0:T(8,128)S(1)}, u32[]{:S(2)}, u32[]{:S(2)}) collective-permute-start(f32[6,2,32,128]{3,2,1,0:T(8,128)S(1)} %get-tuple-element.165), channel_id=1, source_target_pairs={{32,0},{64,32},{96,64},{128,96},{160,128},{192,160},{224,192},{33,... | collective-permute-start | bytes 589832 | tf_op jit(solution)/shard_map/ppermute | solution.py:28
  130.5 7.9 %collective-permute-start.16 = (f32[6,16,2,128]{3,2,1,0:T(2,128)S(1)}, f32[6,16,2,128]{3,2,1,0:T(2,128)S(1)}, u32[]{:S(2)}, u32[]{:S(2)}) collective-permute-start(f32[6,16,2,128]{3,2,1,0:T(2,128)S(1)} %get-tuple-element.163), channel_id=1, source_target_pairs={{0,1},{1,2},{2,3},{3,4},{4,5},{5,6},{6,7},{7,8},{8,9},{9,10},{10,1... | collective-permute-start | bytes 294920 | tf_op jit(solution)/shard_map/ppermute | solution.py:27
  133.0 10.2 %collective-permute-start.19 = (f32[6,16,2,128]{3,2,1,0:T(2,128)S(1)}, f32[6,16,2,128]{3,2,1,0:T(2,128)S(1)}, u32[]{:S(2)}, u32[]{:S(2)}) collective-permute-start(f32[6,16,2,128]{3,2,1,0:T(2,128)S(1)} %get-tuple-element.164), channel_id=1, source_target_pairs={{1,0},{2,1},{3,2},{4,3},{5,4},{6,5},{7,6},{8,7},{9,8},{10,9},{11,1... | collective-permute-start | bytes 294920 | tf_op jit(solution)/shard_map/ppermute | solution.py:28
  227.0 10.3 %collective-permute-start.24 = (f32[2,128,1]{1,2,0:T(1,128)S(1)}, f32[2,128,1]{1,2,0:T(1,128)S(1)}, u32[]{:S(2)}, u32[]{:S(2)}) collective-permute-start(f32[2,128,1]{1,2,0:T(1,128)S(1)} %pad_maximum_fusion.21), channel_id=1, source_target_pairs={{1,0},{2,1},{3,2},{4,3},{5,4},{6,5},{7,6},{8,7},{9,8},{10,9},{11,1... | collective-permute-start | bytes 3080 | tf_op jit(solution)/shard_map/ppermute | solution.py:46
  230.4 7.1 %collective-permute-start.26 = (f32[2,1,256]{2,1,0:T(1,128)S(1)}, f32[2,1,256]{2,1,0:T(1,128)S(1)}, u32[]{:S(2)}, u32[]{:S(2)}) collective-permute-start(f32[2,1,256]{2,1,0:T(1,128)S(1)} %pad_maximum_fusion.20), channel_id=1, source_target_pairs={{32,0},{64,32},{96,64},{128,96},{160,128},{192,160},{224,192},{33,... | collective-permute-start | bytes 6152 | tf_op jit(solution)/shard_map/ppermute | solution.py:46
  239.0 9.2 %collective-permute-start.25 = (f32[128,1]{1,0:T(8,128)S(1)}, f32[128,1]{1,0:T(8,128)S(1)}, u32[]{:S(2)}, u32[]{:S(2)}) collective-permute-start(f32[128,1]{1,0:T(8,128)S(1)} %slice.2008), channel_id=1, source_target_pairs={{0,1},{1,2},{2,3},{3,4},{4,5},{5,6},{6,7},{7,8},{8,9},{9,10},{10,1... | collective-permute-start | bytes 1544 | tf_op jit(solution)/shard_map/ppermute | solution.py:46
  246.1 4.3 %collective-permute-start.27 = (f32[1,256]{1,0:T(1,128)S(1)}, f32[1,256]{1,0:T(1,128)S(1)}, u32[]{:S(2)}, u32[]{:S(2)}) collective-permute-start(f32[1,256]{1,0:T(1,128)S(1)} %slice.2016), channel_id=1, source_target_pairs={{0,32},{32,64},{64,96},{96,128},{128,160},{160,192},{192,224},{1,3... | collective-permute-start | bytes 3080 | tf_op jit(solution)/shard_map/ppermute | solution.py:46
  251.5 18.8 %collective-permute-start.30 = (f32[1,256]{1,0:T(1,128)S(1)}, f32[1,256]{1,0:T(1,128)S(1)}, u32[]{:S(2)}, u32[]{:S(2)}) collective-permute-start(f32[1,256]{1,0:T(1,128)S(1)} %slice.2024), channel_id=1, source_target_pairs={{32,0},{64,32},{96,64},{128,96},{160,128},{192,160},{224,192},{33,... | collective-permute-start | bytes 3080 | tf_op jit(solution)/shard_map/ppermute | solution.py:46
  253.7 16.7 %collective-permute-start.28 = (f32[128,1]{1,0:T(8,128)S(1)}, f32[128,1]{1,0:T(8,128)S(1)}, u32[]{:S(2)}, u32[]{:S(2)}) collective-permute-start(f32[128,1]{1,0:T(8,128)S(1)} %slice.2020), channel_id=1, source_target_pairs={{1,0},{2,1},{3,2},{4,3},{5,4},{6,5},{7,6},{8,7},{9,8},{10,9},{11,1... | collective-permute-start | bytes 1544 | tf_op jit(solution)/shard_map/ppermute | solution.py:46
  255.9 31.6 %collective-permute-start.21 = (f32[3,2,32,128]{3,2,1,0:T(8,128)S(1)}, f32[3,2,32,128]{3,2,1,0:T(8,128)S(1)}, u32[]{:S(2)}, u32[]{:S(2)}) collective-permute-start(f32[3,2,32,128]{3,2,1,0:T(8,128)S(1)} %get-tuple-element.193), channel_id=1, source_target_pairs={{0,32},{32,64},{64,96},{96,128},{128,160},{160,192},{192,224},{1,3... | collective-permute-start | bytes 294920 | tf_op jit(solution)/shard_map/ppermute | solution.py:27
  260.1 27.3 %collective-permute-start.22 = (f32[3,2,32,128]{3,2,1,0:T(8,128)S(1)}, f32[3,2,32,128]{3,2,1,0:T(8,128)S(1)}, u32[]{:S(2)}, u32[]{:S(2)}) collective-permute-start(f32[3,2,32,128]{3,2,1,0:T(8,128)S(1)} %get-tuple-element.194), channel_id=1, source_target_pairs={{32,0},{64,32},{96,64},{128,96},{160,128},{192,160},{224,192},{33,... | collective-permute-start | bytes 294920 | tf_op jit(solution)/shard_map/ppermute | solution.py:28
  262.1 20.1 %collective-permute-start.20 = (f32[3,16,2,128]{3,2,1,0:T(2,128)S(1)}, f32[3,16,2,128]{3,2,1,0:T(2,128)S(1)}, u32[]{:S(2)}, u32[]{:S(2)}) collective-permute-start(f32[3,16,2,128]{3,2,1,0:T(2,128)S(1)} %get-tuple-element.195), channel_id=1, source_target_pairs={{0,1},{1,2},{2,3},{3,4},{4,5},{5,6},{6,7},{7,8},{8,9},{9,10},{10,1... | collective-permute-start | bytes 147464 | tf_op jit(solution)/shard_map/ppermute | solution.py:27
  270.6 7.2 %collective-permute-start.29 = (f32[128,1]{1,0:T(8,128)S(1)}, f32[128,1]{1,0:T(8,128)S(1)}, u32[]{:S(2)}, u32[]{:S(2)}) collective-permute-start(f32[128,1]{1,0:T(8,128)S(1)} %slice.2021), channel_id=1, source_target_pairs={{0,1},{1,2},{2,3},{3,4},{4,5},{5,6},{6,7},{7,8},{8,9},{9,10},{10,1... | collective-permute-start | bytes 1544 | tf_op jit(solution)/shard_map/ppermute | solution.py:46
  272.5 8.0 %collective-permute-start.31 = (f32[1,256]{1,0:T(1,128)S(1)}, f32[1,256]{1,0:T(1,128)S(1)}, u32[]{:S(2)}, u32[]{:S(2)}) collective-permute-start(f32[1,256]{1,0:T(1,128)S(1)} %slice.2025), channel_id=1, source_target_pairs={{0,32},{32,64},{64,96},{96,128},{128,160},{160,192},{192,224},{1,3... | collective-permute-start | bytes 3080 | tf_op jit(solution)/shard_map/ppermute | solution.py:46
  277.8 9.6 %collective-permute-start.23 = (f32[3,16,2,128]{3,2,1,0:T(2,128)S(1)}, f32[3,16,2,128]{3,2,1,0:T(2,128)S(1)}, u32[]{:S(2)}, u32[]{:S(2)}) collective-permute-start(f32[3,16,2,128]{3,2,1,0:T(2,128)S(1)} %get-tuple-element.196), channel_id=1, source_target_pairs={{1,0},{2,1},{3,2},{4,3},{5,4},{6,5},{7,6},{8,7},{9,8},{10,9},{11,1... | collective-permute-start | bytes 147464 | tf_op jit(solution)/shard_map/ppermute | solution.py:28
  (65 other events, 427.6 us)
where the time goes:
time: 297 us; the launch traced here: 294 us
  starting transfers between devices  118 us (40%)
  other arithmetic  72.9 us (25%)
  local copies, waits for them, and re-layouts  38.8 us (13%)
  waiting for transfers between devices  24.7 us (8%)
  blocking collectives  21.1 us (7%)
  matrix products  16.4 us (6%)
    ppermute x12, starting transfers between devices, with_halo(): lax.ppermute(last, axis, up)  63 us
    ppermute x12, starting transfers between devices, with_halo(): lax.ppermute(leading, axis, [(b, a) for a, b in up])  27.4 us
    ppermute x8, starting transfers between devices, passed_along(): return lax.ppermute(x, axis, pairs)  27.3 us
    all_gather x1, blocking collectives, from_root(): lax.all_gather(x, axis)  21.1 us
    ppermute x12, waiting for transfers between devices, with_halo(): lax.ppermute(leading, axis, [(b, a) for a, b in up])  20.7 us
    dot_general x16, matrix products, one_block(): jnp.einsum('rck,kn->rcn', onehot, table, precision=lax.Precision.HIGHEST)  16.4 us
    unnamed x15, other arithmetic  16.1 us
    select_n x16, other arithmetic, one_block(): lower = indices % tile_cols  11.3 us
  transfers between devices with their start and end apart: 32, of which 8 were waited for; matrix products, arithmetic and copies ran while one was open for 7% of the time, Pallas kernels for 0%

commit v1 on v0

v1 whole, which is shorter than its diff:
```python
import jax
import jax.numpy as jnp
from jax import lax
from jax.experimental import pallas as pl
from jax.experimental.pallas import tpu as pltpu
from jax.sharding import PartitionSpec as P

ITERS = 3
OSTEPS = 2

far_coef = 1.0 / 24.0
RATIO = 27.0
time_step = 0.2
ocean_step = 0.2
gravity = 1.0
pull = ocean_step * gravity

LANES = 128
ROW0 = 8
XX, XY, XZ, YZ, ZZ, YY = range(6)
S_DEPTH = ((XZ, YZ + 1, True), (ZZ, ZZ + 1, False))
V_DEPTH = ((0, 2, False), (2, 3, True))
S_MAP = ((XX, False), (XY, True), (XZ, True))
V_MAP = ((0, True), (1, False), (2, False))


def turn_lanes(x, by):
    return pltpu.roll(x, by % LANES, 1)


def fwd(p1, c, p2, m1):
    return p1 - c, p2 - m1


def bwd(c, m1, p1, m2):
    return c - m1, p1 - m2


def fwd_y(f):
    return fwd(turn_lanes(f, -1), f, turn_lanes(f, -2), turn_lanes(f, 1))


def bwd_y(f):
    return bwd(f, turn_lanes(f, 1), turn_lanes(f, -1), turn_lanes(f, 2))


def scaled(*pairs):
    near, far = pairs[0]
    for n, f in pairs[1:]:
        near, far = near + n, far + f
    return RATIO * near - far


def up_slots(fields):
    out = []
    for field, back in fields:
        for k in (2, 1) if back else (1,):
            out.append((field, -k, -k))
    return out


def down_slots(fields):
    out = []
    for field, back in fields:
        for k in (0,) if back else (0, 1):
            out.append((field, k, k))
    return out


def kernel(
    n_depth,
    n_map,
    nz,
    nx,
    rows,
    vel_in,
    str_in,
    reg_in,
    lame_in,
    shear_in,
    buoy_in,
    height_in,
    disch_in,
    face_in,
    wet_in,
    index_in,
    vel_out,
    str_out,
    height_out,
    disch_out,
    S,
    V,
    region,
    dtb,
    dtl,
    dts,
    su_send,
    sd_send,
    su_recv,
    sd_recv,
    vu_send,
    vd_send,
    vu_recv,
    vd_recv,
    tiles,
    level,
    W,
    wet_i,
    index,
    height,
    qx,
    hx,
    fd0,
    qy,
    hy,
    fd1,
    source,
    lift2,
    col_send,
    col_recv,
    qw,
    hw,
    lame_t,
    shear_t,
    buoy_t,
    in_sem,
    out_sem,
    s_send_sem,
    s_recv_sem,
    v_send_sem,
    v_recv_sem,
    t_send_sem,
    t_recv_sem,
    o_send_sem,
    o_recv_sem,
):
    d = lax.axis_index("depth")
    m = lax.axis_index("map")
    has_low, has_high = d > 0, d < n_depth - 1
    has_west, has_east = m > 0, m < n_map - 1
    low, high = {"depth": d - 1, "map": m}, {"depth": d + 1, "map": m}
    west, east = {"depth": d, "map": m - 1}, {"depth": d, "map": m + 1}
    sides = ((has_low, low), (has_high, high), (has_west, west), (has_east, east))
    f32 = jnp.float32
    halves = range(2)

    s_loads = [
        pltpu.make_async_copy(
            str_in.at[f], S.at[f, pl.ds(2, nz), pl.ds(ROW0, nx), :], in_sem.at[f]
        )
        for f in range(6)
    ]
    r_loads = [
        pltpu.make_async_copy(src, dst, in_sem.at[k])
        for src, dst, k in (
            (reg_in, region, 6),
            (lame_in, lame_t, 24),
            (shear_in, shear_t, 25),
            (buoy_in, buoy_t, 26),
        )
    ]
    v_loads = [
        pltpu.make_async_copy(
            vel_in.at[f], V.at[f, pl.ds(2, nz), pl.ds(ROW0, nx), :], in_sem.at[7 + f]
        )
        for f in range(3)
    ]
    o_loads = []

    def half_load(src, dst):
        o_loads.append(pltpu.make_async_copy(src, dst, in_sem.at[10 + len(o_loads)]))

    for h in halves:
        cols = pl.ds(h * LANES, LANES)
        half_load(wet_in.at[:, cols], wet_i.at[h])
        half_load(index_in.at[:, cols], index.at[h])
        half_load(height_in.at[:, cols], height.at[h])
        half_load(disch_in.at[0, :, cols], qx.at[h])
        half_load(disch_in.at[1, :, cols], qy.at[h, pl.ds(8, rows), :])
        half_load(face_in.at[0, :, cols], fd0.at[h])
        half_load(face_in.at[1, :, cols], fd1.at[h, pl.ds(8, rows), :])
    for c in s_loads + r_loads + v_loads + o_loads:
        c.start()

    def clear_layers(z):
        for f in (XZ, YZ, ZZ):
            S[f, pl.ds(z, 2), pl.ds(ROW0, nx), :] = jnp.zeros((2, nx, LANES), f32)
        for f in range(3):
            V[f, pl.ds(z, 2), pl.ds(ROW0, nx), :] = jnp.zeros((2, nx, LANES), f32)

    @pl.when(d == 0)
    def _():
        clear_layers(0)

    @pl.when(d == n_depth - 1)
    def _():
        clear_layers(nz + 2)

    @pl.when(m == 0)
    def _():
        for ref in (su_recv, vu_recv):
            ref[...] = jnp.zeros(ref.shape, f32)

    @pl.when(m == n_map - 1)
    def _():
        for ref in (sd_recv, vd_recv):
            ref[...] = jnp.zeros(ref.shape, f32)

    for h in halves:
        for t in range(OSTEPS):
            level[t, h, pl.ds(0, 8), :] = jnp.zeros((8, LANES), f32)
            level[t, h, pl.ds(rows + 8, 8), :] = jnp.zeros((8, LANES), f32)
        W[h, pl.ds(0, 8), :] = jnp.zeros((8, LANES), f32)
        W[h, pl.ds(rows + 8, 8), :] = jnp.zeros((8, LANES), f32)
        qy[h, pl.ds(0, 8), :] = jnp.zeros((8, LANES), f32)
        fd1[h, pl.ds(0, 8), :] = jnp.zeros((8, LANES), f32)
    for k in range(3 + OSTEPS):
        col_recv[k] = jnp.zeros((LANES, LANES), f32)

    barrier = pltpu.get_barrier_semaphore()
    for there, who in sides:
        @pl.when(there)
        def _():
            pl.semaphore_signal(barrier, inc=1, device_id=who, device_id_type=pl.DeviceIdType.MESH)

    @pl.when(d > 1)
    def _():
        pl.semaphore_signal(
            barrier, inc=1, device_id={"depth": 0, "map": m}, device_id_type=pl.DeviceIdType.MESH
        )

    peers = sum(there.astype(jnp.int32) for there, _who in sides)
    pl.semaphore_wait(barrier, peers + jnp.where(d == 0, max(n_depth - 2, 0), 0))

    def remote(src, dst, ssem, rsem, who):
        return pltpu.make_async_remote_copy(
            src_ref=src,
            dst_ref=dst,
            send_sem=ssem,
            recv_sem=rsem,
            device_id=who,
            device_id_type=pl.DeviceIdType.MESH,
        )

    def over(lo, hi, body, at_once=1):
        def step(i, _):
            for k in range(at_once):
                body(lo + i * at_once + k)
            return 0

        lax.fori_loop(0, (hi - lo) // at_once, step, 0)

    xs = pl.ds(ROW0, nx)

    def depth_copies(ref, fields, ssem, rsem):
        ups, downs = [], []
        for k, (lo, hi, back) in enumerate(fields):
            n_up, n_down = (2, 1) if back else (1, 2)
            fs = pl.ds(lo, hi - lo)
            ups.append(
                remote(
                    ref.at[fs, pl.ds(nz + 2 - n_up, n_up), xs, :],
                    ref.at[fs, pl.ds(2 - n_up, n_up), xs, :],
                    ssem.at[k],
                    rsem.at[k],
                    high,
                )
            )
            downs.append(
                remote(
                    ref.at[fs, pl.ds(2, n_down), xs, :],
                    ref.at[fs, pl.ds(nz + 2, n_down), xs, :],
                    ssem.at[2 + k],
                    rsem.at[2 + k],
                    low,
                )
            )
        return ups, downs

    s_up, s_down = depth_copies(S, S_DEPTH, s_send_sem, s_recv_sem)
    v_up, v_down = depth_copies(V, V_DEPTH, v_send_sem, v_recv_sem)
    s_east = [remote(su_send, su_recv, s_send_sem.at[4], s_recv_sem.at[4], east)]
    s_west = [remote(sd_send, sd_recv, s_send_sem.at[5], s_recv_sem.at[5], west)]
    v_east = [remote(vu_send, vu_recv, v_send_sem.at[4], v_recv_sem.at[4], east)]
    v_west = [remote(vd_send, vd_recv, v_send_sem.at[5], v_recv_sem.at[5], west)]
    S_PLAN = (S, S_MAP, s_up, s_down, s_east, s_west, su_send, sd_send, su_recv, sd_recv)
    V_PLAN = (V, V_MAP, v_up, v_down, v_east, v_west, vu_send, vd_send, vu_recv, vd_recv)

    def each(there, copies, what):
        @pl.when(there)
        def _():
            for c in copies:
                getattr(c, what)()

    def send_depth(plan):
        each(has_high, plan[2], "start")
        each(has_low, plan[3], "start")

    def send_map(plan):
        ref, fields, _, _, east_c, west_c, u_send, d_send, _, _ = plan

        def pack(i):
            for j, (f, row, _r) in enumerate(up_slots(fields)):
                u_send[j, pl.ds(i, 1), :] = ref[f, i + 2, pl.ds(ROW0 + nx + row, 1), :]
            for j, (f, row, _r) in enumerate(down_slots(fields)):
                d_send[j, pl.ds(i, 1), :] = ref[f, i + 2, pl.ds(ROW0 + row, 1), :]

        over(0, nz, pack, 4)
        each(has_east, east_c, "start")
        each(has_west, west_c, "start")

    def take_map(plan):
        ref, fields, _, _, east_c, west_c, _, _, u_recv, d_recv = plan

        each(has_west, east_c, "wait_recv")
        each(has_east, west_c, "wait_recv")

        def unpack(i):
            for j, (f, _row, row) in enumerate(up_slots(fields)):
                ref[f, i + 2, pl.ds(ROW0 + row, 1), :] = u_recv[j, pl.ds(i, 1), :]
            for j, (f, _row, row) in enumerate(down_slots(fields)):
                ref[f, i + 2, pl.ds(ROW0 + nx + row, 1), :] = d_recv[j, pl.ds(i, 1), :]

        over(0, nz, unpack, 4)

    def take_depth(plan):
        each(has_low, plan[2], "wait_recv")
        each(has_high, plan[3], "wait_recv")

    def wait_sends(plan):
        each(has_high, plan[2], "wait_send")
        each(has_low, plan[3], "wait_send")
        each(has_east, plan[4], "wait_send")
        each(has_west, plan[5], "wait_send")

    def velocity_rows(z, a, b):
        def s(f, dz, dx):
            return S[f, z + 2 + dz, pl.ds(ROW0 + a + dx, b - a), :]

        def v_add(f, total):
            at = (f, z + 2, pl.ds(ROW0 + a, b - a), slice(None))
            V[at] = V[at] + dtb[z, pl.ds(a, b - a), :] * total

        xy, xz, yz = s(XY, 0, 0), s(XZ, 0, 0), s(YZ, 0, 0)
        v_add(
            0,
            scaled(
                fwd(s(XX, 0, 1), s(XX, 0, 0), s(XX, 0, 2), s(XX, 0, -1)),
                bwd_y(xy),
                bwd(xz, s(XZ, -1, 0), s(XZ, 1, 0), s(XZ, -2, 0)),
            ),
        )
        v_add(
            1,
            scaled(
                bwd(xy, s(XY, 0, -1), s(XY, 0, 1), s(XY, 0, -2)),
                fwd_y(s(YY, 0, 0)),
                bwd(yz, s(YZ, -1, 0), s(YZ, 1, 0), s(YZ, -2, 0)),
            ),
        )
        v_add(
            2,
            scaled(
                bwd(xz, s(XZ, 0, -1), s(XZ, 0, 1), s(XZ, 0, -2)),
                bwd_y(yz),
                fwd(s(ZZ, 1, 0), s(ZZ, 0, 0), s(ZZ, 2, 0), s(ZZ, -1, 0)),
            ),
        )

    def stress_rows(z, a, b):
        def v(f, dz, dx):
            return V[f, z + 2 + dz, pl.ds(ROW0 + a + dx, b - a), :]

        def s_add(f, change):
            at = (f, z + 2, pl.ds(ROW0 + a, b - a), slice(None))
            S[at] = S[at] + change

        x, y, w = v(0, 0, 0), v(1, 0, 0), v(2, 0, 0)
        ex = scaled(bwd(x, v(0, 0, -1), v(0, 0, 1), v(0, 0, -2)))
        ey = scaled(bwd_y(y))
        ez = scaled(bwd(w, v(2, -1, 0), v(2, 1, 0), v(2, -2, 0)))
        mu = dts[z, pl.ds(a, b - a), :]
        both = dtl[z, pl.ds(a, b - a), :] * (ex + ey + ez)
        mu2 = mu + mu
        s_add(XX, both + mu2 * ex)
        s_add(YY, both + mu2 * ey)
        s_add(ZZ, both + mu2 * ez)
        s_add(XY, mu * scaled(fwd_y(x), fwd(v(1, 0, 1), y, v(1, 0, 2), v(1, 0, -1))))
        s_add(
            XZ,
            mu
            * scaled(
                fwd(v(0, 1, 0), x, v(0, 2, 0), v(0, -1, 0)),
                fwd(v(2, 0, 1), w, v(2, 0, 2), v(2, 0, -1)),
            ),
        )
        s_add(YZ, mu * scaled(fwd(v(1, 1, 0), y, v(1, 2, 0), v(1, -1, 0)), fwd_y(w)))

    def inner(rows_of):
        over(2, nz - 2, lambda z: rows_of(z, 8, nx - 8), 2)

    def beside(rows_of):
        def body(z):
            rows_of(z, 0, 8)
            rows_of(z, nx - 8, nx)

        over(2, nz - 2, body, 2)

    def outer(rows_of):
        def body(i):
            rows_of(i, 0, nx)
            rows_of(i + nz - 2, 0, nx)

        over(0, 2, body)

    for c in s_loads:
        c.wait()
    send_depth(S_PLAN)
    send_map(S_PLAN)

    for c in r_loads:
        c.wait()
    lame = [lame_t[k] * (time_step * far_coef) for k in range(8)]
    shear = [shear_t[k] * (time_step * far_coef) for k in range(8)]
    buoy = [buoy_t[k] * (time_step * far_coef) for k in range(8)]

    def material(z):
        r = region[z]
        bit0, bit1, bit2 = (r & 1) > 0, (r & 2) > 0, (r & 4) > 0
        for table, out in ((lame, dtl), (shear, dts), (buoy, dtb)):
            a = [jnp.where(bit0, table[2 * k + 1], table[2 * k]) for k in range(4)]
            b = [jnp.where(bit1, a[2 * k + 1], a[2 * k]) for k in range(2)]
            out[z] = jnp.where(bit2, b[1], b[0])

    over(0, nz, material)
    for c in v_loads:
        c.wait()

    lane = lax.broadcasted_iota(jnp.int32, (rows, LANES), 1)
    first, last = lane == 0, lane == LANES - 1
    own = pl.ds(8, rows)

    def row_copies(ref, k, both):
        out = [
            (
                has_high,
                has_low,
                remote(
                    ref.at[:, pl.ds(rows, 8), :],
                    ref.at[:, pl.ds(0, 8), :],
                    o_send_sem.at[k],
                    o_recv_sem.at[k],
                    high,
                ),
            )
        ]
        if both:
            out.append(
                (
                    has_low,
                    has_high,
                    remote(
                        ref.at[:, pl.ds(8, 8), :],
                        ref.at[:, pl.ds(rows + 8, 8), :],
                        o_send_sem.at[k + 1],
                        o_recv_sem.at[k + 1],
                        low,
                    ),
                )
            )
        return out

    def col_copies(slot, k, both):
        tail = pl.ds(LANES - 8, 8)
        out = [
            (
                has_east,
                has_west,
                remote(
                    col_send.at[slot, tail, :],
                    col_recv.at[slot, tail, :],
                    o_send_sem.at[k],
                    o_recv_sem.at[k],
                    east,
                ),
            )
        ]
        if both:
            head = pl.ds(0, 8)
            out.append(
                (
                    has_west,
                    has_east,
                    remote(
                        col_send.at[slot, head, :],
                        col_recv.at[slot, head, :],
                        o_send_sem.at[k + 1],
                        o_recv_sem.at[k + 1],
                        west,
                    ),
                )
            )
        return out

    def start_all(copies):
        for there, _from, c in copies:
            each(there, [c], "start")

    def recv_all(copies):
        for _there, came, c in copies:
            each(came, [c], "wait_recv")

    def sent_all(copies):
        for there, _from, c in copies:
            each(there, [c], "wait_send")

    for c in o_loads:
        c.wait()
    for h in halves:
        W[h, own, :] = wet_i[h].astype(f32)
    col_send[0] = jnp.where(first, W[0, own, :], W[1, own, :]).T
    col_send[1] = fd0[1].T
    col_send[2] = qx[1].T
    fixed = (
        row_copies(W, 0, True)
        + row_copies(fd1, 2, False)
        + row_copies(qy, 3, False)
        + col_copies(0, 4, True)
        + col_copies(1, 6, False)
        + col_copies(2, 7, False)
    )
    start_all(fixed)

    def east_of(x0, x1, edge):
        r1 = turn_lanes(x1, -1)
        return (
            jnp.where(last, r1, turn_lanes(x0, -1)),
            jnp.where(last, turn_lanes(edge, -1), r1),
        )

    def west_of(x0, x1, edge):
        r0 = turn_lanes(x0, 1)
        return (
            jnp.where(first, turn_lanes(edge, 1), r0),
            jnp.where(first, r0, turn_lanes(x1, 1)),
        )

    def ocean_fixed():
        recv_all(fixed)
        sent_all(fixed)
        edge = col_recv[0].T
        w = (W[0, own, :], W[1, own, :])
        w_east = east_of(w[0], w[1], edge)
        wide = pl.ds(0, rows + 8)
        for h in halves:
            mask = w[h] * w_east[h]
            hx[h] = fd0[h] * mask
            qx[h] = qx[h] * mask
            mask = W[h, wide, :] * W[h, pl.ds(1, rows + 8), :]
            hy[h] = fd1[h] * mask
            qy[h] = qy[h] * mask
        mask = edge * turn_lanes(w[0], -1)
        hw[...] = col_recv[1].T * mask
        qw[...] = col_recv[2].T * mask

    def tile_copies(k):
        return [
            remote(
                tiles.at[k],
                tiles.at[k],
                t_send_sem.at[k * (n_depth - 1) + i],
                t_recv_sem.at[k],
                {"depth": i + 1, "map": m},
            )
            for i in range(n_depth - 1)
        ]

    sends = [tile_copies(0), tile_copies(1)]

    def send_tile(k):
        if n_depth > 1:
            each(d == 0, sends[k], "start")

    def take_tile(k):
        if n_depth > 1:
            each(d > 0, sends[k][:1], "wait_recv")

    def pick(k, take):
        def body(i):
            at = pl.ds(i * 8, 8)
            where = [index[h, at, :] for h in halves]
            lane_at = [x & (LANES - 1) for x in where]
            row_at = [x >> 7 for x in where]
            found = [[], []]
            for r in range(nx):
                line = jnp.broadcast_to(tiles[k, pl.ds(r, 1), :], (8, LANES))
                for h in halves:
                    found[h].append(
                        jnp.take_along_axis(line, lane_at[h], axis=1, wrap_negative_indices=False)
                    )
            for h in halves:
                level_found, bit = found[h], 1
                while len(level_found) > 1:
                    odd = (row_at[h] & bit) > 0
                    level_found = [
                        jnp.where(odd, level_found[j + 1], level_found[j])
                        for j in range(0, len(level_found), 2)
                    ]
                    bit *= 2
                take(h, at, level_found[0])

        over(0, rows // 8, body)

    for turn in range(ITERS):
        inner(velocity_rows)
        take_map(S_PLAN)
        beside(velocity_rows)
        take_depth(S_PLAN)
        outer(velocity_rows)
        if turn == ITERS - 1:
            @pl.when(d == 0)
            def _():
                tiles[1] = V[2, 2, xs, :]
            send_tile(1)
        send_depth(V_PLAN)
        send_map(V_PLAN)
        if turn < ITERS - 1:
            @pl.when(d == 0)
            def _():
                now = time_step * V[2, 2, xs, :]
                tiles[0] = now if turn == 0 else tiles[0] + now
            if turn == ITERS - 2:
                send_tile(0)
        wait_sends(S_PLAN)
        if turn == 0:
            ocean_fixed()
        inner(stress_rows)
        if turn == ITERS - 1:
            break
        take_map(V_PLAN)
        beside(stress_rows)
        take_depth(V_PLAN)
        outer(stress_rows)
        send_depth(S_PLAN)
        send_map(S_PLAN)
        wait_sends(V_PLAN)
        if turn == ITERS - 2:
            take_tile(0)
            def keep(h, at, found):
                lift2[h, at, :] = found

            pick(0, keep)

    v_store = pltpu.make_async_copy(V.at[:, pl.ds(2, nz), xs, :], vel_out, out_sem.at[0])
    v_store.start()

    take_tile(1)
    def begin(h, at, rate):
        here = pl.ds(at.start + 8, 8)
        w = W[h, here, :]
        level[0, h, here, :] = w * (height[h, at, :] + (lift2[h, at, :] + time_step * rate))
        source[h, at, :] = w * rate

    pick(1, begin)
    levels = [
        row_copies(level.at[t], 8 + 4 * t, True) + col_copies(3 + t, 10 + 4 * t, True)
        for t in range(OSTEPS)
    ]

    def send_level(t):
        col_send[3 + t] = jnp.where(first, level[t, 0, own, :], level[t, 1, own, :]).T
        start_all(levels[t])

    send_level(0)

    take_map(V_PLAN)
    beside(stress_rows)
    take_depth(V_PLAN)
    outer(stress_rows)
    s_store = pltpu.make_async_copy(S.at[:, pl.ds(2, nz), xs, :], str_out, out_sem.at[1])
    s_store.start()
    wait_sends(V_PLAN)

    for turn in range(OSTEPS):
        recv_all(levels[turn])
        sent_all(levels[turn])
        edge = col_recv[3 + turn].T
        L = level.at[turn]
        now = (L[0, own, :], L[1, own, :])
        ahead = east_of(now[0], now[1], edge)
        qw[...] = qw[...] - pull * hw[...] * (turn_lanes(now[0], -1) - edge)
        for h in halves:
            qx[h] = qx[h] - pull * hx[h] * (ahead[h] - now[h])
            qy[h] = qy[h] - pull * hy[h] * (
                L[h, pl.ds(1, rows + 8), :] - L[h, pl.ds(0, rows + 8), :]
            )
        behind = west_of(qx[0], qx[1], qw[...])
        for h in halves:
            new = (
                now[h]
                - ocean_step
                * W[h, own, :]
                * (
                    (qx[h] - behind[h])
                    + (qy[h, own, :] - qy[h, pl.ds(7, rows), :])
                )
                + ocean_step * source[h]
            )
            if turn < OSTEPS - 1:
                level[turn + 1, h, own, :] = new
            else:
                height[h] = new
        if turn < OSTEPS - 1:
            send_level(turn + 1)

    stores = []
    for h in halves:
        cols = pl.ds(h * LANES, LANES)
        for src, dst in (
            (height.at[h], height_out.at[:, cols]),
            (qx.at[h], disch_out.at[0, :, cols]),
            (qy.at[h, own, :], disch_out.at[1, :, cols]),
        ):
            stores.append(pltpu.make_async_copy(src, dst, out_sem.at[2 + len(stores)]))
            stores[-1].start()
    if n_depth > 1:
        for k in range(2):
            each(d == 0, sends[k], "wait_send")
    for c in [v_store, s_store] + stores:
        c.wait()


def solution(mesh):
    n_depth, n_map = mesh.shape["depth"], mesh.shape["map"]

    def per_device(*args):
        velocity, stress, height, discharge = args[0], args[1], args[6], args[7]
        nz, nx = velocity.shape[1], velocity.shape[2]
        rows = height.shape[0]
        f32 = jnp.float32
        hbm = pl.BlockSpec(memory_space=pltpu.HBM)
        any_space = pl.BlockSpec(memory_space=pl.ANY)

        def vm(*shape, dtype=f32):
            return pltpu.VMEM(shape, dtype)

        halves = vm(2, rows, LANES)
        ints = vm(2, rows, LANES, dtype=jnp.int32)
        low_pad = vm(2, rows + 8, LANES)
        padded = vm(2, rows + 16, LANES)
        n_up = len(up_slots(S_MAP))
        n_down = len(down_slots(S_MAP))
        n_vup = len(up_slots(V_MAP))
        n_vdown = len(down_slots(V_MAP))
        dma = pltpu.SemaphoreType.DMA
        scratch = [
            vm(6, nz + 4, nx + 16, LANES),
            vm(3, nz + 4, nx + 16, LANES),
            vm(nz, nx, LANES, dtype=jnp.int32),
            vm(nz, nx, LANES),
            vm(nz, nx, LANES),
            vm(nz, nx, LANES),
            vm(n_up, nz, LANES),
            vm(n_down, nz, LANES),
            vm(n_up, nz, LANES),
            vm(n_down, nz, LANES),
            vm(n_vup, nz, LANES),
            vm(n_vdown, nz, LANES),
            vm(n_vup, nz, LANES),
            vm(n_vdown, nz, LANES),
            vm(2, nx, LANES),
            vm(OSTEPS, 2, rows + 16, LANES),
            padded,
            ints,
            ints,
            halves,
            halves,
            halves,
            halves,
            low_pad,
            low_pad,
            low_pad,
            halves,
            halves,
            vm(3 + OSTEPS, LANES, LANES),
            vm(3 + OSTEPS, LANES, LANES),
            vm(LANES, LANES),
            vm(LANES, LANES),
        ]
        scratch += [pltpu.SMEM(args[k].shape, f32) for k in (3, 4, 5)]
        scratch += [
            dma((28,)),
            dma((8,)),
            dma((6,)),
            dma((6,)),
            dma((6,)),
            dma((6,)),
            dma((2 * max(n_depth - 1, 1),)),
            dma((2,)),
            dma((8 + 4 * OSTEPS,)),
            dma((8 + 4 * OSTEPS,)),
        ]

        def body(*refs):
            kernel(n_depth, n_map, nz, nx, rows, *refs)

        shapes = tuple(
            jax.ShapeDtypeStruct(x.shape, f32) for x in (velocity, stress, height, discharge)
        )
        results = pl.pallas_call(
            body,
            out_shape=shapes,
            in_specs=[hbm] * len(args),
            out_specs=(any_space,) * 4,
            scratch_shapes=scratch,
            compiler_params=pltpu.CompilerParams(
                collective_id=0, has_side_effects=True, vmem_limit_bytes=32 * 1024 * 1024
            ),
        )(*[pltpu.with_memory_space_constraint(x, pltpu.HBM) for x in args])

        def deliver(*refs):
            copies = [
                pltpu.make_async_copy(refs[k], refs[4 + k], refs[8].at[k]) for k in range(4)
            ]
            for c in copies:
                c.start()
            for c in copies:
                c.wait()

        return pl.pallas_call(
            deliver,
            out_shape=shapes,
            in_specs=[any_space] * 4,
            out_specs=(hbm,) * 4,
            scratch_shapes=[dma((4,))],
            compiler_params=pltpu.CompilerParams(vmem_limit_bytes=1024 * 1024),
        )(*results)

    return jax.shard_map(
        per_device,
        mesh=mesh,
        in_specs=(
            P(None, "depth", "map", None),
            P(None, "depth", "map", None),
            P("depth", "map", None),
            P(),
            P(),
            P(),
            P("depth", "map"),
            P(None, "depth", "map"),
            P(None, "depth", "map"),
            P("depth", "map"),
            P("depth", "map"),
        ),
        out_specs=(
            P(None, "depth", "map", None),
            P(None, "depth", "map", None),
            P("depth", "map"),
            P(None, "depth", "map"),
        ),
        check_vma=False,
    )
```

time: 297 us -> 54.9 us (0.18)
  starting transfers between devices: 118 us -> 0 us
  other arithmetic: 72.9 us -> 0 us
  Pallas kernels: 0 us -> 53.2 us
  local copies, waits for them, and re-layouts: 38.8 us -> 0 us
  waiting for transfers between devices: 24.7 us -> 0 us
  blocking collectives: 21.1 us -> 0 us
  matrix products: 16.4 us -> 0 us
    ppermute x32 -> x0, starting transfers between devices: 118 us -> none  [the longest x12 63 us: with_halo(): lax.ppermute(last, axis, up)]
    pallas_call x0 -> x2, Pallas kernels: none -> 53.2 us  [the longest x1 51.6 us: per_device(): pl.pallas_call(body, out_shape=shapes, in_specs=[hbm] * len(args), out_sp...]
    slice x77 -> x0, local copies, waits for them, and re-layouts: 28.4 us -> none  [the longest x10 6.96 us: forward_y(): jnp.roll(field, 1, 2)]
    ppermute x32 -> x0, waiting for transfers between devices: 24.7 us -> none  [the longest x12 20.7 us: with_halo(): lax.ppermute(leading, axis, [(b, a) for a, b in up])]
    select_n x32 -> x0, other arithmetic: 22.6 us -> none  [the longest x16 11.3 us: one_block(): lower = indices % tile_cols]
    all_gather x1 -> x0, blocking collectives: 21.1 us -> none  [from_root(): lax.all_gather(x, axis)]
    dot_general x16 -> x0, matrix products: 16.4 us -> none  [one_block(): jnp.einsum('rck,kn->rcn', onehot, table, precision=lax.Precision.HIGHEST)]
    unnamed x15 -> x0, other arithmetic: 16.1 us -> none
  transfers between devices with their start and end apart: 32 -> 0, of which waited for: 8 -> 0; matrix products, arithmetic and copies ran while one was open for 7% -> 0% of each run, Pallas kernels for 0% -> 0%
where the time goes in v1:
time: 54.9 us; the launch traced here: 53.8 us
  Pallas kernels  53.2 us (97%)
  between operations  0.64 us (1%)
    pallas_call x1, Pallas kernels, per_device(): pl.pallas_call(body, out_shape=shapes, in_specs=[hbm] * len(args), out_sp...  51.6 us
    pallas_call x1, Pallas kernels, per_device(): pl.pallas_call(deliver, out_shape=shapes, in_specs=[any_space] * 4, out_s...  1.56 us

profile of v1, /device:TPU:121, one launch (start us, length us, event | category | flops | bytes accessed | tf_op | source)
XLA Modules:
  0.0 53.8 jit_solution(7634220682160744454)
XLA Ops:
  0.6 51.6 %shard_map.138 = (f32[3,16,32,128]{3,2,1,0:T(8,128)S(1)}, f32[6,16,32,128]{3,2,1,0:T(8,128)S(1)}, f32[128,256]{1,0:T(8,128)S(1)}, f32[2,128,256]{2,1,0:T(8,128)S(1)}) custom-call(f32[3,16,32,128]{3,2,1,0:T(8,128)} %refs_0_.1, f32[6,16,32,128]{3,2,1,0:T(8,128)} %refs_1_.1, s32[16,32,128]{2,1,0:T(8,128)} %refs_2_.1, f32[8]{0:T(128)} %refs_3_.1, f32[8]{0:T(128)} %refs_4_.1, ...), custom_call_target="tpu_custom_call" | custom-call | tf_op jit(solution)/shard_map/pallas_call | solution.py:810
  52.2 1.6 %shard_map.139 = (f32[3,16,32,128]{3,2,1,0:T(8,128)}, f32[6,16,32,128]{3,2,1,0:T(8,128)}, f32[128,256]{1,0:T(8,128)}, f32[2,128,256]{2,1,0:T(8,128)}) custom-call(f32[3,16,32,128]{3,2,1,0:T(8,128)S(1)} %get-tuple-element.8.refs_0_, f32[6,16,32,128]{3,2,1,0:T(8,128)S(1)} %get-tuple-element.9.refs_1_, f32[128,256]{1,0:T(8,128)S(1)} %get-tuple-element.10.refs_2_, ...), custom_call_target="tpu_custom_call" | custom-call | tf_op jit(solution)/shard_map/pallas_call | solution.py:830

commit v2 on v1

--- a/solution.py
+++ b/solution.py
@@ -65,6 +65,9 @@
         for k in (0,) if back else (0, 1):
             out.append((field, k, k))
     return out
+
+
+N_ROWS = 9
 
 
 def kernel(
@@ -94,14 +97,10 @@
     dtb,
     dtl,
     dts,
-    su_send,
-    sd_send,
-    su_recv,
-    sd_recv,
-    vu_send,
-    vd_send,
-    vu_recv,
-    vd_recv,
+    s_mid,
+    s_end,
+    v_mid,
+    v_end,
     tiles,
     level,
     W,
@@ -196,15 +195,12 @@
     def _():
         clear_layers(nz + 2)
 
-    @pl.when(m == 0)
-    def _():
-        for ref in (su_recv, vu_recv):
-            ref[...] = jnp.zeros(ref.shape, f32)
-
-    @pl.when(m == n_map - 1)
-    def _():
-        for ref in (sd_recv, vd_recv):
-            ref[...] = jnp.zeros(ref.shape, f32)
+    for there in (m == 0, m == n_map - 1):
+        @pl.when(there)
+        def _():
+            for ref in (s_mid, s_end, v_mid, v_end):
+                for j in range(N_ROWS):
+                    ref[1, j] = jnp.zeros(ref.shape[2:], f32)
 
     for h in halves:
         for t in range(OSTEPS):
@@ -279,12 +275,22 @@
 
     s_up, s_down = depth_copies(S, S_DEPTH, s_send_sem, s_recv_sem)
     v_up, v_down = depth_copies(V, V_DEPTH, v_send_sem, v_recv_sem)
-    s_east = [remote(su_send, su_recv, s_send_sem.at[4], s_recv_sem.at[4], east)]
-    s_west = [remote(sd_send, sd_recv, s_send_sem.at[5], s_recv_sem.at[5], west)]
-    v_east = [remote(vu_send, vu_recv, v_send_sem.at[4], v_recv_sem.at[4], east)]
-    v_west = [remote(vd_send, vd_recv, v_send_sem.at[5], v_recv_sem.at[5], west)]
-    S_PLAN = (S, S_MAP, s_up, s_down, s_east, s_west, su_send, sd_send, su_recv, sd_recv)
-    V_PLAN = (V, V_MAP, v_up, v_down, v_east, v_west, vu_send, vd_send, vu_recv, vd_recv)
+
+    def map_copies(fields, buf, ssem, rsem, k):
+        n_up = len(up_slots(fields))
+        ups, downs = pl.ds(0, n_up), pl.ds(n_up, N_ROWS - n_up)
+        return (
+            [remote(buf.at[0, ups], buf.at[1, ups], ssem.at[k], rsem.at[k], east)],
+            [remote(buf.at[0, downs], buf.at[1, downs], ssem.at[k + 1], rsem.at[k + 1], west)],
+        )
+
+    end_layers = [0, 1, nz - 2, nz - 1]
+    S_PLAN = dict(ref=S, fields=S_MAP, up=s_up, down=s_down)
+    S_PLAN["mid"] = (s_mid, map_copies(S_MAP, s_mid, s_send_sem, s_recv_sem, 4))
+    S_PLAN["end"] = (s_end, map_copies(S_MAP, s_end, s_send_sem, s_recv_sem, 6))
+    V_PLAN = dict(ref=V, fields=V_MAP, up=v_up, down=v_down)
+    V_PLAN["mid"] = (v_mid, map_copies(V_MAP, v_mid, v_send_sem, v_recv_sem, 4))
+    V_PLAN["end"] = (v_end, map_copies(V_MAP, v_end, v_send_sem, v_recv_sem, 6))
 
     def each(there, copies, what):
         @pl.when(there)
@@ -293,130 +299,143 @@
                 getattr(c, what)()
 
     def send_depth(plan):
-        each(has_high, plan[2], "start")
-        each(has_low, plan[3], "start")
-
-    def send_map(plan):
-        ref, fields, _, _, east_c, west_c, u_send, d_send, _, _ = plan
-
-        def pack(i):
-            for j, (f, row, _r) in enumerate(up_slots(fields)):
-                u_send[j, pl.ds(i, 1), :] = ref[f, i + 2, pl.ds(ROW0 + nx + row, 1), :]
-            for j, (f, row, _r) in enumerate(down_slots(fields)):
-                d_send[j, pl.ds(i, 1), :] = ref[f, i + 2, pl.ds(ROW0 + row, 1), :]
-
-        over(0, nz, pack, 4)
-        each(has_east, east_c, "start")
-        each(has_west, west_c, "start")
-
-    def take_map(plan):
-        ref, fields, _, _, east_c, west_c, _, _, u_recv, d_recv = plan
-
-        each(has_west, east_c, "wait_recv")
-        each(has_east, west_c, "wait_recv")
-
-        def unpack(i):
-            for j, (f, _row, row) in enumerate(up_slots(fields)):
-                ref[f, i + 2, pl.ds(ROW0 + row, 1), :] = u_recv[j, pl.ds(i, 1), :]
-            for j, (f, _row, row) in enumerate(down_slots(fields)):
-                ref[f, i + 2, pl.ds(ROW0 + nx + row, 1), :] = d_recv[j, pl.ds(i, 1), :]
-
-        over(0, nz, unpack, 4)
-
-    def take_depth(plan):
-        each(has_low, plan[2], "wait_recv")
-        each(has_high, plan[3], "wait_recv")
+        each(has_high, plan["up"], "start")
+        each(has_low, plan["down"], "start")
+
+    def over_layers(part, body):
+        if part == "mid":
+            over(2, nz - 2, lambda z: body(z, z - 2), 4)
+        else:
+            for i, z in enumerate(end_layers):
+                body(z, i)
+
+    def send_map(plan, part):
+        ref, (buf, (eastward, westward)) = plan["ref"], plan[part]
+        n_up = len(up_slots(plan["fields"]))
+
+        def pack(z, i):
+            for j, (f, row, _r) in enumerate(up_slots(plan["fields"])):
+                buf[0, j, pl.ds(i, 1), :] = ref[f, z + 2, pl.ds(ROW0 + nx + row, 1), :]
+            for j, (f, row, _r) in enumerate(down_slots(plan["fields"])):
+                buf[0, n_up + j, pl.ds(i, 1), :] = ref[f, z + 2, pl.ds(ROW0 + row, 1), :]
+
+        over_layers(part, pack)
+        each(has_east, eastward, "start")
+        each(has_west, westward, "start")
+
+    def take_map(plan, part):
+        ref, (buf, (eastward, westward)) = plan["ref"], plan[part]
+        n_up = len(up_slots(plan["fields"]))
+        each(has_west, eastward, "wait_recv")
+        each(has_east, westward, "wait_recv")
+
+        def unpack(z, i):
+            for j, (f, _row, row) in enumerate(up_slots(plan["fields"])):
+                ref[f, z + 2, pl.ds(ROW0 + row, 1), :] = buf[1, j, pl.ds(i, 1), :]
+            for j, (f, _row, row) in enumerate(down_slots(plan["fields"])):
+                ref[f, z + 2, pl.ds(ROW0 + nx + row, 1), :] = buf[1, n_up + j, pl.ds(i, 1), :]
+
+        over_layers(part, unpack)
+
+    def take_low(plan):
+        each(has_low, plan["up"], "wait_recv")
+
+    def take_high(plan):
+        each(has_high, plan["down"], "wait_recv")
 
     def wait_sends(plan):
-        each(has_high, plan[2], "wait_send")
-        each(has_low, plan[3], "wait_send")
-        each(has_east, plan[4], "wait_send")
-        each(has_west, plan[5], "wait_send")
-
-    def velocity_rows(z, a, b):
+        each(has_high, plan["up"], "wait_send")
+        each(has_low, plan["down"], "wait_send")
+        for part in ("mid", "end"):
+            each(has_east, plan[part][1][0], "wait_send")
+            each(has_west, plan[part][1][1], "wait_send")
+
+    def velocity_rows(z, a, b, along):
         def s(f, dz, dx):
             return S[f, z + 2 + dz, pl.ds(ROW0 + a + dx, b - a), :]
 
-        def v_add(f, total):
+        parts = [[], [], []]
+        if "y" in along:
+            parts[0].append(bwd_y(s(XY, 0, 0)))
+            parts[1].append(fwd_y(s(YY, 0, 0)))
+            parts[2].append(bwd_y(s(YZ, 0, 0)))
+        if "x" in along:
+            parts[0].append(fwd(s(XX, 0, 1), s(XX, 0, 0), s(XX, 0, 2), s(XX, 0, -1)))
+            parts[1].append(bwd(s(XY, 0, 0), s(XY, 0, -1), s(XY, 0, 1), s(XY, 0, -2)))
+            parts[2].append(bwd(s(XZ, 0, 0), s(XZ, 0, -1), s(XZ, 0, 1), s(XZ, 0, -2)))
+        if "z" in along:
+            parts[0].append(bwd(s(XZ, 0, 0), s(XZ, -1, 0), s(XZ, 1, 0), s(XZ, -2, 0)))
+            parts[1].append(bwd(s(YZ, 0, 0), s(YZ, -1, 0), s(YZ, 1, 0), s(YZ, -2, 0)))
+            parts[2].append(fwd(s(ZZ, 1, 0), s(ZZ, 0, 0), s(ZZ, 2, 0), s(ZZ, -1, 0)))
+        scale = dtb[z, pl.ds(a, b - a), :]
+        for f in range(3):
             at = (f, z + 2, pl.ds(ROW0 + a, b - a), slice(None))
-            V[at] = V[at] + dtb[z, pl.ds(a, b - a), :] * total
-
-        xy, xz, yz = s(XY, 0, 0), s(XZ, 0, 0), s(YZ, 0, 0)
-        v_add(
-            0,
-            scaled(
-                fwd(s(XX, 0, 1), s(XX, 0, 0), s(XX, 0, 2), s(XX, 0, -1)),
-                bwd_y(xy),
-                bwd(xz, s(XZ, -1, 0), s(XZ, 1, 0), s(XZ, -2, 0)),
-            ),
-        )
-        v_add(
-            1,
-            scaled(
-                bwd(xy, s(XY, 0, -1), s(XY, 0, 1), s(XY, 0, -2)),
-                fwd_y(s(YY, 0, 0)),
-                bwd(yz, s(YZ, -1, 0), s(YZ, 1, 0), s(YZ, -2, 0)),
-            ),
-        )
-        v_add(
-            2,
-            scaled(
-                bwd(xz, s(XZ, 0, -1), s(XZ, 0, 1), s(XZ, 0, -2)),
-                bwd_y(yz),
-                fwd(s(ZZ, 1, 0), s(ZZ, 0, 0), s(ZZ, 2, 0), s(ZZ, -1, 0)),
-            ),
-        )
-
-    def stress_rows(z, a, b):
+            V[at] = V[at] + scale * scaled(*parts[f])
+
+    def stress_rows(z, a, b, along):
         def v(f, dz, dx):
             return V[f, z + 2 + dz, pl.ds(ROW0 + a + dx, b - a), :]
 
-        def s_add(f, change):
+        x, y, w = v(0, 0, 0), v(1, 0, 0), v(2, 0, 0)
+        own = {}
+        shears = {XY: [], XZ: [], YZ: []}
+        if "y" in along:
+            own[YY] = scaled(bwd_y(y))
+            shears[XY].append(fwd_y(x))
+            shears[YZ].append(fwd_y(w))
+        if "x" in along:
+            own[XX] = scaled(bwd(x, v(0, 0, -1), v(0, 0, 1), v(0, 0, -2)))
+            shears[XY].append(fwd(v(1, 0, 1), y, v(1, 0, 2), v(1, 0, -1)))
+            shears[XZ].append(fwd(v(2, 0, 1), w, v(2, 0, 2), v(2, 0, -1)))
+        if "z" in along:
+            own[ZZ] = scaled(bwd(w, v(2, -1, 0), v(2, 1, 0), v(2, -2, 0)))
+            shears[XZ].append(fwd(v(0, 1, 0), x, v(0, 2, 0), v(0, -1, 0)))
+            shears[YZ].append(fwd(v(1, 1, 0), y, v(1, 2, 0), v(1, -1, 0)))
+        mu = dts[z, pl.ds(a, b - a), :]
+        both = dtl[z, pl.ds(a, b - a), :] * sum(list(own.values())[1:], list(own.values())[0])
+        mu2 = mu + mu
+        changes = {f: both + mu2 * own[f] if f in own else both for f in (XX, YY, ZZ)}
+        changes.update({f: mu * scaled(*p) for f, p in shears.items() if p})
+        for f, change in changes.items():
             at = (f, z + 2, pl.ds(ROW0 + a, b - a), slice(None))
             S[at] = S[at] + change
 
-        x, y, w = v(0, 0, 0), v(1, 0, 0), v(2, 0, 0)
-        ex = scaled(bwd(x, v(0, 0, -1), v(0, 0, 1), v(0, 0, -2)))
-        ey = scaled(bwd_y(y))
-        ez = scaled(bwd(w, v(2, -1, 0), v(2, 1, 0), v(2, -2, 0)))
-        mu = dts[z, pl.ds(a, b - a), :]
-        both = dtl[z, pl.ds(a, b - a), :] * (ex + ey + ez)
-        mu2 = mu + mu
-        s_add(XX, both + mu2 * ex)
-        s_add(YY, both + mu2 * ey)
-        s_add(ZZ, both + mu2 * ez)
-        s_add(XY, mu * scaled(fwd_y(x), fwd(v(1, 0, 1), y, v(1, 0, 2), v(1, 0, -1))))
-        s_add(
-            XZ,
-            mu
-            * scaled(
-                fwd(v(0, 1, 0), x, v(0, 2, 0), v(0, -1, 0)),
-                fwd(v(2, 0, 1), w, v(2, 0, 2), v(2, 0, -1)),
-            ),
-        )
-        s_add(YZ, mu * scaled(fwd(v(1, 1, 0), y, v(1, 2, 0), v(1, -1, 0)), fwd_y(w)))
-
-    def inner(rows_of):
-        over(2, nz - 2, lambda z: rows_of(z, 8, nx - 8), 2)
-
-    def beside(rows_of):
+    def local(rows_of):
+        def body(z, along):
+            rows_of(z, 0, 8, along)
+            rows_of(z, 8, nx - 8, along + "x")
+            rows_of(z, nx - 8, nx, along)
+
+        over(2, nz - 2, lambda z: body(z, "yz"))
+
+        def ends(i):
+            body(i, "y")
+            body(i + nz - 2, "y")
+
+        over(0, 2, ends)
+
+    def after_map(rows_of, part):
         def body(z):
-            rows_of(z, 0, 8)
-            rows_of(z, nx - 8, nx)
-
-        over(2, nz - 2, body, 2)
-
-    def outer(rows_of):
-        def body(i):
-            rows_of(i, 0, nx)
-            rows_of(i + nz - 2, 0, nx)
-
-        over(0, 2, body)
+            rows_of(z, 0, 8, "x")
+            rows_of(z, nx - 8, nx, "x")
+
+        if part == "mid":
+            over(2, nz - 2, body, 2)
+        else:
+            over(0, 2, body)
+            over(nz - 2, nz, body)
+
+    def after_low(rows_of):
+        over(0, 2, lambda z: rows_of(z, 0, nx, "z"))
+
+    def after_high(rows_of):
+        over(nz - 2, nz, lambda z: rows_of(z, 0, nx, "z"))
 
     for c in s_loads:
         c.wait()
+    send_map(S_PLAN, "mid")
+    send_map(S_PLAN, "end")
     send_depth(S_PLAN)
-    send_map(S_PLAN)
 
     for c in r_loads:
         c.wait()
@@ -609,21 +628,26 @@
                     bit *= 2
                 take(h, at, level_found[0])
 
-        over(0, rows // 8, body)
+        over(0, rows // 8, body, 2)
 
     for turn in range(ITERS):
-        inner(velocity_rows)
-        take_map(S_PLAN)
-        beside(velocity_rows)
-        take_depth(S_PLAN)
-        outer(velocity_rows)
+        local(velocity_rows)
+        take_map(S_PLAN, "mid")
+        after_map(velocity_rows, "mid")
+        send_map(V_PLAN, "mid")
+        take_map(S_PLAN, "end")
+        after_map(velocity_rows, "end")
+        take_low(S_PLAN)
+        after_low(velocity_rows)
         if turn == ITERS - 1:
             @pl.when(d == 0)
             def _():
                 tiles[1] = V[2, 2, xs, :]
             send_tile(1)
+        take_high(S_PLAN)
+        after_high(velocity_rows)
+        send_map(V_PLAN, "end")
         send_depth(V_PLAN)
-        send_map(V_PLAN)
         if turn < ITERS - 1:
             @pl.when(d == 0)
             def _():
@@ -632,20 +656,26 @@
             if turn == ITERS - 2:
                 send_tile(0)
         wait_sends(S_PLAN)
+        local(stress_rows)
         if turn == 0:
             ocean_fixed()
-        inner(stress_rows)
         if turn == ITERS - 1:
             break
-        take_map(V_PLAN)
-        beside(stress_rows)
-        take_depth(V_PLAN)
-        outer(stress_rows)
+        take_map(V_PLAN, "mid")
+        after_map(stress_rows, "mid")
+        send_map(S_PLAN, "mid")
+        take_map(V_PLAN, "end")
+        after_map(stress_rows, "end")
+        take_low(V_PLAN)
+        after_low(stress_rows)
+        take_high(V_PLAN)
+        after_high(stress_rows)
+        send_map(S_PLAN, "end")
         send_depth(S_PLAN)
-        send_map(S_PLAN)
         wait_sends(V_PLAN)
         if turn == ITERS - 2:
             take_tile(0)
+
             def keep(h, at, found):
                 lift2[h, at, :] = found
 
@@ -673,27 +703,39 @@
 
     send_level(0)
 
-    take_map(V_PLAN)
-    beside(stress_rows)
-    take_depth(V_PLAN)
-    outer(stress_rows)
+    for part in ("mid", "end"):
+        take_map(V_PLAN, part)
+        after_map(stress_rows, part)
+    take_low(V_PLAN)
+    after_low(stress_rows)
+    take_high(V_PLAN)
+    after_high(stress_rows)
     s_store = pltpu.make_async_copy(S.at[:, pl.ds(2, nz), xs, :], str_out, out_sem.at[1])
     s_store.start()
     wait_sends(V_PLAN)
 
     for turn in range(OSTEPS):
-        recv_all(levels[turn])
-        sent_all(levels[turn])
-        edge = col_recv[3 + turn].T
         L = level.at[turn]
         now = (L[0, own, :], L[1, own, :])
-        ahead = east_of(now[0], now[1], edge)
+
+        def flow_x(h, ahead):
+            qx[h] = qx[h] - pull * hx[h] * (ahead - now[h])
+
+        def flow_y(at, n):
+            for h in halves:
+                here = pl.ds(at, n)
+                qy[h, here, :] = qy[h, here, :] - pull * hy[h, here, :] * (
+                    L[h, pl.ds(at + 1, n), :] - L[h, here, :]
+                )
+
+        flow_x(0, east_of(now[0], now[1], now[1])[0])
+        flow_y(8, rows - 8)
+        recv_all(levels[turn])
+        edge = col_recv[3 + turn].T
+        flow_x(1, east_of(now[0], now[1], edge)[1])
+        flow_y(0, 8)
+        flow_y(rows, 8)
         qw[...] = qw[...] - pull * hw[...] * (turn_lanes(now[0], -1) - edge)
-        for h in halves:
-            qx[h] = qx[h] - pull * hx[h] * (ahead[h] - now[h])
-            qy[h] = qy[h] - pull * hy[h] * (
-                L[h, pl.ds(1, rows + 8), :] - L[h, pl.ds(0, rows + 8), :]
-            )
         behind = west_of(qx[0], qx[1], qw[...])
         for h in halves:
             new = (
@@ -723,6 +765,8 @@
         ):
             stores.append(pltpu.make_async_copy(src, dst, out_sem.at[2 + len(stores)]))
             stores[-1].start()
+    for copies in levels:
+        sent_all(copies)
     if n_depth > 1:
         for k in range(2):
             each(d == 0, sends[k], "wait_send")
@@ -748,10 +792,6 @@
         ints = vm(2, rows, LANES, dtype=jnp.int32)
         low_pad = vm(2, rows + 8, LANES)
         padded = vm(2, rows + 16, LANES)
-        n_up = len(up_slots(S_MAP))
-        n_down = len(down_slots(S_MAP))
-        n_vup = len(up_slots(V_MAP))
-        n_vdown = len(down_slots(V_MAP))
         dma = pltpu.SemaphoreType.DMA
         scratch = [
             vm(6, nz + 4, nx + 16, LANES),
@@ -760,14 +800,10 @@
             vm(nz, nx, LANES),
             vm(nz, nx, LANES),
             vm(nz, nx, LANES),
-            vm(n_up, nz, LANES),
-            vm(n_down, nz, LANES),
-            vm(n_up, nz, LANES),
-            vm(n_down, nz, LANES),
-            vm(n_vup, nz, LANES),
-            vm(n_vdown, nz, LANES),
-            vm(n_vup, nz, LANES),
-            vm(n_vdown, nz, LANES),
+            vm(2, N_ROWS, nz - 4, LANES),
+            vm(2, N_ROWS, 4, LANES),
+            vm(2, N_ROWS, nz - 4, LANES),
+            vm(2, N_ROWS, 4, LANES),
             vm(2, nx, LANES),
             vm(OSTEPS, 2, rows + 16, LANES),
             padded,
@@ -791,10 +827,10 @@
         scratch += [
             dma((28,)),
             dma((8,)),
-            dma((6,)),
-            dma((6,)),
-            dma((6,)),
-            dma((6,)),
+            dma((8,)),
+            dma((8,)),
+            dma((8,)),
+            dma((8,)),
             dma((2 * max(n_depth - 1, 1),)),
             dma((2,)),
             dma((8 + 4 * OSTEPS,)),

time: 54.9 us -> 49.1 us (0.89); the launches traced: 53.8 us -> 48.9 us
  Pallas kernels: 53.2 us -> 48.3 us
    pallas_call x1, Pallas kernels: 51.6 us -> 46.7 us  [per_device(): pl.pallas_call(body, out_shape=shapes, in_specs=[hbm] * len(args), out_sp...]
where the time goes in v2:
time: 49.1 us; the launch traced here: 48.9 us
  Pallas kernels  48.3 us (98%)
  between operations  0.64 us (1%)
    pallas_call x1, Pallas kernels, per_device(): pl.pallas_call(body, out_shape=shapes, in_specs=[hbm] * len(args), out_sp...  46.7 us
    pallas_call x1, Pallas kernels, per_device(): pl.pallas_call(deliver, out_shape=shapes, in_specs=[any_space] * 4, out_s...  1.56 us

profile of v2, /device:TPU:121, one launch (start us, length us, event | category | flops | bytes accessed | tf_op | source)
XLA Modules:
  0.0 48.9 jit_solution(5516019065836879485)
XLA Ops:
  0.6 46.7 %shard_map.138 = (f32[3,16,32,128]{3,2,1,0:T(8,128)S(1)}, f32[6,16,32,128]{3,2,1,0:T(8,128)S(1)}, f32[128,256]{1,0:T(8,128)S(1)}, f32[2,128,256]{2,1,0:T(8,128)S(1)}) custom-call(f32[3,16,32,128]{3,2,1,0:T(8,128)} %refs_0_.1, f32[6,16,32,128]{3,2,1,0:T(8,128)} %refs_1_.1, s32[16,32,128]{2,1,0:T(8,128)} %refs_2_.1, f32[8]{0:T(128)} %refs_3_.1, f32[8]{0:T(128)} %refs_4_.1, ...), custom_call_target="tpu_custom_call" | custom-call | tf_op jit(solution)/shard_map/pallas_call | solution.py:846
  47.4 1.6 %shard_map.139 = (f32[3,16,32,128]{3,2,1,0:T(8,128)}, f32[6,16,32,128]{3,2,1,0:T(8,128)}, f32[128,256]{1,0:T(8,128)}, f32[2,128,256]{2,1,0:T(8,128)}) custom-call(f32[3,16,32,128]{3,2,1,0:T(8,128)S(1)} %get-tuple-element.8.refs_0_, f32[6,16,32,128]{3,2,1,0:T(8,128)S(1)} %get-tuple-element.9.refs_1_, f32[128,256]{1,0:T(8,128)S(1)} %get-tuple-element.10.refs_2_, ...), custom_call_target="tpu_custom_call" | custom-call | tf_op jit(solution)/shard_map/pallas_call | solution.py:866
